TPU v7x, 256 devices: a whole 4x4x8 slice. The times are simulated.
256 devices in a mesh: outer: 8 (over y, core), inner: 32 (over x, z).
Axes of the slice: x: 4, y: 4, z: 8, core: 2. Of those that a mesh axis runs over, the one named last changes fastest.
Arguments:
- query_rows: bfloat16 [65536, 1024], P(('outer', 'inner')), may hold values from -6 to 6
- key_rows: bfloat16 [65536, 1024], P(('outer', 'inner')), may hold values from -6 to 6
- value_rows: bfloat16 [65536, 1024], P(('outer', 'inner')), may hold values from -6 to 6
- log_decay: float32 [8, 65536], P(None, ('outer', 'inner')), may hold values from -0.8 to 0, as said below
- grad_out: bfloat16 [65536, 1024], P(('outer', 'inner')), may hold values from -6 to 6
Outputs:
- attended: bfloat16 [65536, 1024], P(('outer', 'inner'))
- grad_queries: bfloat16 [65536, 1024], P(('outer', 'inner'))
- grad_keys: bfloat16 [65536, 1024], P(('outer', 'inner'))
- grad_values: bfloat16 [65536, 1024], P(('outer', 'inner'))
Inputs may be any that keep to these rules, and one draw needn't show every extreme that they name: `log_decay`: every entry is negative.
All inputs are finite; a program needn't handle non-finite values.
Results may differ from a plain program's by a relative error of at most 0.0063.
Values sent between devices are 32-bit elements; how exact they have to be, the bound alone decides.
No kernel may reach another device: no remote copies, remote signals or barrier semaphores. Data moves between devices by JAX's collectives and lax.ppermute only.
A program may use at most 320 MiB of HBM per device.

v0:
```python
import math

import jax
import jax.numpy as jnp
from jax import lax
from jax.sharding import Mesh
from jax.sharding import PartitionSpec as P

OUTER_INNER = ("outer_0", "outer_1", "inner_0", "inner_1")


EPSILON = 1e-06


def nothing_yet(array, identity):
    return jax.tree.map(
        lambda part, zero: jnp.zeros_like(part) + jnp.asarray(zero, part.dtype), array, identity
    )


def prefix_by_axis(array, axes, combine, identity, reverse):
    before = start = nothing_yet(array, identity)
    so_far = array
    for axis in reversed(axes):
        size, place = (lax.axis_size(axis), lax.axis_index(axis))
        pieces = jax.tree.map(lambda part: lax.all_gather(part, axis), so_far)
        inside, so_far = (start, start)
        for k in reversed(range(size)) if reverse else range(size):
            passed = k > place if reverse else k < place
            so_far = combine(so_far, jax.tree.map(lambda part: part[k], pieces))
            inside = jax.tree.map(lambda new, old: jnp.where(passed, new, old), so_far, inside)
        before = combine(inside, before)
    return before


def combine(earlier, latter):
    return (earlier[0] + latter[0], jnp.exp(latter[0])[:, None, None] * earlier[1] + latter[1])


def carried(states, backward):
    identity = (jnp.zeros_like(states[0]), jnp.zeros_like(states[1]))
    return prefix_by_axis(states, OUTER_INNER, combine, identity, backward)


def causal_decay(running):
    length_rows = running.shape[1]
    row_index = lax.broadcasted_iota(jnp.int32, (length_rows, length_rows), 0)
    col_index = lax.broadcasted_iota(jnp.int32, (length_rows, length_rows), 1)
    causal = (col_index <= row_index)[None]
    gaps = running[:, :, None] - running[:, None, :]
    return jnp.where(causal, jnp.exp(jnp.where(causal, gaps, 0.0)), 0.0)


def body(query_rows, key_rows, value_rows, log_decay, grad_out):
    head_count = log_decay.shape[0]
    length_rows = log_decay.shape[1]
    head_size = query_rows.shape[1] // head_count
    scaling = 1.0 / math.sqrt(head_size)
    block_shape = (length_rows, head_count, head_size)
    queries = query_rows.reshape(block_shape)
    keys_local = key_rows.reshape(block_shape)
    values = value_rows.reshape(block_shape)
    running = jnp.cumsum(log_decay, axis=1)
    totals = running[:, -1]
    growth = jnp.exp(running).T[:, :, None]
    shrink = jnp.exp(totals[:, None] - running).T[:, :, None]
    query_dec = (queries.astype(jnp.float32) * growth).astype(jnp.bfloat16)
    key_dec = (keys_local.astype(jnp.float32) * shrink).astype(jnp.bfloat16)
    block_state = jnp.einsum("the,thf->hef", key_dec, values, preferred_element_type=jnp.float32)
    _, entering = carried((totals, block_state), False)
    decay_mat = causal_decay(running)
    scores = jnp.einsum("the,she->hts", queries, keys_local, preferred_element_type=jnp.float32)
    weights = (scores * scaling * decay_mat).astype(jnp.bfloat16)
    entering_half = entering.astype(jnp.bfloat16)
    mixed = jnp.einsum("hts,shf->thf", weights, values, preferred_element_type=jnp.float32)
    mixed = mixed + scaling * jnp.einsum(
        "the,hef->thf", query_dec, entering_half, preferred_element_type=jnp.float32
    )
    inverse = lax.rsqrt(jnp.mean(mixed * mixed, axis=2, keepdims=True) + EPSILON)
    normed = mixed * inverse
    grad_normed = grad_out.reshape(block_shape).astype(jnp.float32)
    grad_mixed = (
        inverse * (grad_normed - normed * jnp.mean(grad_normed * normed, axis=2, keepdims=True))
    ).astype(jnp.bfloat16)
    back_state = scaling * jnp.einsum(
        "the,thf->hef", query_dec, grad_mixed, preferred_element_type=jnp.float32
    )
    _, leaving = carried((totals, back_state), True)
    grad_prob = jnp.einsum("thf,shf->hts", grad_mixed, values, preferred_element_type=jnp.float32)
    grad_score = (grad_prob * scaling * decay_mat).astype(jnp.bfloat16)
    grad_q = jnp.einsum("hts,she->the", grad_score, keys_local, preferred_element_type=jnp.float32)
    grad_q = grad_q + scaling * growth * jnp.einsum(
        "thf,hef->the", grad_mixed, entering_half, preferred_element_type=jnp.float32
    )
    grad_v = jnp.einsum("hts,thf->shf", weights, grad_mixed, preferred_element_type=jnp.float32)
    grad_k = jnp.einsum("hts,the->she", grad_score, queries, preferred_element_type=jnp.float32)
    leaving_half = leaving.astype(jnp.bfloat16)
    grad_k = grad_k + shrink * jnp.einsum(
        "shf,hef->she", values, leaving_half, preferred_element_type=jnp.float32
    )
    grad_v = grad_v + jnp.einsum(
        "she,hef->shf", key_dec, leaving_half, preferred_element_type=jnp.float32
    )
    attended = normed.astype(jnp.bfloat16).reshape(length_rows, -1)
    return (
        attended,
        grad_q.astype(jnp.bfloat16).reshape(length_rows, -1),
        grad_k.astype(jnp.bfloat16).reshape(length_rows, -1),
        grad_v.astype(jnp.bfloat16).reshape(length_rows, -1),
    )


def solution(mesh):
    finer = Mesh(mesh.devices.reshape(4, 2, 4, 8), ("outer_0", "outer_1", "inner_0", "inner_1"))
    placed = (
        P(OUTER_INNER, None),
        P(OUTER_INNER, None),
        P(OUTER_INNER, None),
        P(None, OUTER_INNER),
        P(OUTER_INNER, None),
    )
    return jax.shard_map(
        body,
        mesh=finer,
        in_specs=placed,
        out_specs=(
            P(OUTER_INNER, None),
            P(OUTER_INNER, None),
            P(OUTER_INNER, None),
            P(OUTER_INNER, None),
        ),
        check_vma=False,
    )
```

profile of v0, /device:TPU:32, one launch (start us, length us, event | category | flops | bytes accessed | tf_op | source)
XLA Modules:
  0.0 325.1 jit_solution(12609348167315833636)
XLA Ops:
  13.0 17.9 %all-reduce = f32[64]{0:T(128)S(1)} all-reduce(f32[64]{0:T(128)S(1)} %dynamic-update-slice), channel_id=2, replica_groups=mesh['outer_0'=4,'outer_1'=2,'inner_0'=4,'inner_1'=8] {'inner_1'}, use_global_device_ids=true, to_apply=%add | all-reduce | flops 64 | bytes 512
  31.6 35.7 %all-gather.30.cloned.1.call-done = f32[64,128,128]{2,1,0:T(8,128)} async-done(((f32[8,128,128]{2,1,0:T(8,128)}), f32[64,128,128]{2,1,0:T(8,128)}) %all-gather.30.cloned.1.call-update) | async-done | bytes 4194320 | tf_op jit(solution)/shard_map/all_gather | solution.py:26
  67.2 3.3 %bitcast_add_fusion.20 = f32[1,8,128,128]{3,2,1,0:T(8,128)} fusion(f32[64,128,128]{2,1,0:T(8,128)} %all-gather.30.cloned.1.call-done, f32[8]{0:T(128)S(1)} %get-tuple-element.61, f32[8]{0:T(128)S(1)} %get-tuple-element.68, f32[8]{0:T(128)S(1)} %get-tuple-element.67, f32[8]{0:T(128)S(1)} %get-tuple-element.66, f32[8]{0:T(128)S(1)} %get-tuple-element.65, ...), kind=kLoop, calls=%fused_computation.94 | loop fusion | flops 1966080 | bytes 4718848 | tf_op jit(solution)/shard_map/add | solution.py:37
  71.3 9.6 %all-gather.3 = f32[4,1,8]{2,1,0:T(1,128)S(1)} all-gather(f32[1,1,8]{2,1,0:T(1,128)S(1)} %get-tuple-element.59), channel_id=1, replica_groups=mesh['outer_0'=4,'outer_1'=2,'inner_0'=4,'inner_1'=8] {'inner_0'}, dimensions={0}, use_global_device_ids=true | all-gather | bytes 160 | tf_op jit(solution)/shard_map/all_gather | solution.py:26
  80.9 23.7 %all-gather.18.cloned.1.call-done = f32[4,8,128,128]{3,2,1,0:T(8,128)} async-done(((f32[1,8,128,128]{3,2,1,0:T(8,128)}), f32[4,8,128,128]{3,2,1,0:T(8,128)}) %all-gather.18.cloned.1.call-update) | async-done | bytes 2097168 | tf_op jit(solution)/shard_map/all_gather | solution.py:26
  104.5 2.6 multiply_add_fusion.3
  107.2 1.9 all-gather.4
  109.1 12.6 %all-gather.20.cloned.1.call-done = f32[2,8,128,128]{3,2,1,0:T(8,128)} async-done(((f32[1,8,128,128]{3,2,1,0:T(8,128)}), f32[2,8,128,128]{3,2,1,0:T(8,128)}) %all-gather.20.cloned.1.call-update) | async-done | bytes 1048592 | tf_op jit(solution)/shard_map/all_gather | solution.py:26
  121.7 2.1 multiply_add_fusion.2
  124.6 9.6 %all-gather.5 = f32[4,1,8]{2,1,0:T(1,128)S(1)} all-gather(f32[1,1,8]{2,1,0:T(1,128)S(1)} %get-tuple-element.29), channel_id=1, replica_groups=mesh['outer_0'=4,'outer_1'=2,'inner_0'=4,'inner_1'=8] {'outer_0'}, dimensions={0}, use_global_device_ids=true | all-gather | bytes 160 | tf_op jit(solution)/shard_map/all_gather | solution.py:26
  139.1 19.7 %all-gather.22.cloned.1.call-done = f32[4,8,128,128]{3,2,1,0:T(8,128)} async-done(((f32[1,8,128,128]{3,2,1,0:T(8,128)}), f32[4,8,128,128]{3,2,1,0:T(8,128)}) %all-gather.22.cloned.1.call-update) | async-done | bytes 2097168 | tf_op jit(solution)/shard_map/all_gather | solution.py:26
  158.8 4.7 %fusion.26 = bf16[8,128,128]{2,1,0:T(8,128)(2,1)S(1)} fusion(f32[4,8,128,128]{3,2,1,0:T(8,128)} %all-gather.22.cloned.1.call-done, f32[2,8,128,128]{3,2,1,0:T(8,128)} %all-gather.20.cloned.1.call-done, f32[4,8,128,128]{3,2,1,0:T(8,128)} %all-gather.18.cloned.1.call-done, f32[64,128,128]{2,1,0:T(8,128)} %all-gather.30.cloned.1.call-done, f32[8]{0:T(128)S(1)} %copy-done.17, ...), kind=kLoop, calls=%fused_computation.48 | loop fusion | flops 7471104 | bytes 9700018 | tf_op jit(solution)/shard_map/convert_element_type | solution.py:74
  166.3 53.2 %all-gather.32.cloned.1.call-done = f32[64,128,128]{2,1,0:T(8,128)} async-done(((f32[8,128,128]{2,1,0:T(8,128)}), f32[64,128,128]{2,1,0:T(8,128)}) %all-gather.32.cloned.1.call-update) | async-done | bytes 4194320 | tf_op jit(solution)/shard_map/all_gather | solution.py:26
  219.5 3.3 %bitcast_add_fusion.6 = f32[1,8,128,128]{3,2,1,0:T(8,128)} fusion(f32[64,128,128]{2,1,0:T(8,128)} %all-gather.32.cloned.1.call-done, f32[8]{0:T(128)S(1)} %copy-done.14, f32[8]{0:T(128)S(1)} %copy-done.12, f32[8]{0:T(128)S(1)} %get-tuple-element.68, f32[8]{0:T(128)S(1)} %get-tuple-element.67, f32[8]{0:T(128)S(1)} %get-tuple-element.66, ...), kind=kLoop, calls=%fused_computation.67 | loop fusion | flops 1966080 | bytes 4718848 | tf_op jit(solution)/shard_map/add | solution.py:37
  222.9 9.6 %all-gather.6 = f32[4,1,8]{2,1,0:T(1,128)S(1)} all-gather(f32[1,1,8]{2,1,0:T(1,128)S(1)} %copy-done.26), channel_id=1, replica_groups=mesh['outer_0'=4,'outer_1'=2,'inner_0'=4,'inner_1'=8] {'inner_0'}, dimensions={0}, use_global_device_ids=true | all-gather | bytes 160 | tf_op jit(solution)/shard_map/all_gather | solution.py:26
  232.5 24.2 %all-gather.24.cloned.1.call-done = f32[4,8,128,128]{3,2,1,0:T(8,128)} async-done(((f32[1,8,128,128]{3,2,1,0:T(8,128)}), f32[4,8,128,128]{3,2,1,0:T(8,128)}) %all-gather.24.cloned.1.call-update) | async-done | bytes 2097168 | tf_op jit(solution)/shard_map/all_gather | solution.py:26
  256.8 2.5 multiply_add_fusion.1
  261.2 12.8 %all-gather.26.cloned.1.call-done = f32[2,8,128,128]{3,2,1,0:T(8,128)} async-done(((f32[1,8,128,128]{3,2,1,0:T(8,128)}), f32[2,8,128,128]{3,2,1,0:T(8,128)}) %all-gather.26.cloned.1.call-update) | async-done | bytes 1048592 | tf_op jit(solution)/shard_map/all_gather | solution.py:26
  273.9 2.1 multiply_add_fusion
  276.7 9.8 %all-gather.8 = f32[4,1,8]{2,1,0:T(1,128)S(1)} all-gather(f32[1,1,8]{2,1,0:T(1,128)S(1)} %get-tuple-element.21), channel_id=1, replica_groups=mesh['outer_0'=4,'outer_1'=2,'inner_0'=4,'inner_1'=8] {'outer_0'}, dimensions={0}, use_global_device_ids=true | all-gather | bytes 160 | tf_op jit(solution)/shard_map/all_gather | solution.py:26
  292.2 2.6 fusion.89
  294.8 2.5 convolution_bitcast_fusion.2
  297.3 13.7 %all-gather.28.cloned.1.call-done = f32[4,8,128,128]{3,2,1,0:T(8,128)} async-done(((f32[1,8,128,128]{3,2,1,0:T(8,128)}), f32[4,8,128,128]{3,2,1,0:T(8,128)}) %all-gather.28.cloned.1.call-update) | async-done | bytes 2097168 | tf_op jit(solution)/shard_map/all_gather | solution.py:26
  311.1 4.4 %fusion.18 = bf16[8,128,128]{2,1,0:T(8,128)(2,1)S(1)} fusion(f32[4,8,128,128]{3,2,1,0:T(8,128)} %all-gather.28.cloned.1.call-done, f32[2,8,128,128]{3,2,1,0:T(8,128)S(1)} %copy-done.1, f32[4,8,128,128]{3,2,1,0:T(8,128)} %all-gather.24.cloned.1.call-done, f32[64,128,128]{2,1,0:T(8,128)} %all-gather.32.cloned.1.call-done, f32[8]{0:T(128)S(1)} %copy-done.15, ...), kind=kLoop, calls=%fused_computation.36 | loop fusion | flops 7471104 | bytes 9700018 | tf_op jit(solution)/shard_map/convert_element_type | solution.py:97
  (127 shorter events, 25.5 us)
Async XLA Ops:
  7.2 60.1 %all-gather.30.cloned.1.call-start = ((), (), s32[]{:S(2)}) async-start(), calls=%async_computation.6 | async-start | bytes 4718592 | tf_op jit(solution)/shard_map/all_gather | solution.py:26
  11.5 93.1 %all-gather.18.cloned.1.call-start = ((), (), s32[]{:S(2)}) async-start(), calls=%async_computation | async-start | bytes 2621440 | tf_op jit(solution)/shard_map/all_gather | solution.py:26
  31.6 39.0 %copy-start.16 = (f32[8]{0:T(128)}, f32[8]{0:T(128)S(1)}, u32[]{:S(2)}) copy-start(f32[8]{0:T(128)S(1)} %get-tuple-element.61) | copy-start | bytes 100
  31.6 39.0 %copy-start.18 = (f32[8]{0:T(128)}, f32[8]{0:T(128)S(1)}, u32[]{:S(2)}) copy-start(f32[8]{0:T(128)S(1)} %get-tuple-element.69) | copy-start | bytes 100
  70.6 51.1 %all-gather.20.cloned.1.call-start = ((), (), s32[]{:S(2)}) async-start(), calls=%async_computation.1 | async-start | bytes 1572864 | tf_op jit(solution)/shard_map/all_gather | solution.py:26
  104.5 30.8 %copy-start.9 = (bf16[256,1024]{1,0:T(8,128)(2,1)S(1)}, bf16[256,1024]{1,0:T(8,128)(2,1)}, u32[]{:S(2)}) copy-start(bf16[256,1024]{1,0:T(8,128)(2,1)} %param.5) | copy-start | bytes 1572868
  107.1 28.4 %copy-start.8 = (bf16[256,1024]{1,0:T(8,128)(2,1)S(1)}, bf16[256,1024]{1,0:T(8,128)(2,1)}, u32[]{:S(2)}) copy-start(bf16[256,1024]{1,0:T(8,128)(2,1)} %param.9) | copy-start | bytes 1572868
  107.2 51.6 %all-gather.22.cloned.1.call-start = ((), (), s32[]{:S(2)}) async-start(), calls=%async_computation.2 | async-start | bytes 2621440 | tf_op jit(solution)/shard_map/all_gather | solution.py:26
  109.1 26.4 %copy-start.10 = (f32[8]{0:T(128)}, f32[8]{0:T(128)S(1)}, u32[]{:S(2)}) copy-start(f32[8]{0:T(128)S(1)} %get-tuple-element.57) | copy-start | bytes 100
  123.9 95.6 %all-gather.32.cloned.1.call-start = ((), (), s32[]{:S(2)}) async-start(), calls=%async_computation.7 | async-start | bytes 4718592 | tf_op jit(solution)/shard_map/all_gather | solution.py:26
  137.6 21.2 %copy-start.11 = (f32[8]{0:T(128)S(1)}, f32[8]{0:T(128)}, u32[]{:S(2)}) copy-start(f32[8]{0:T(128)} %copy-done.10) | copy-start | bytes 100
  137.6 21.2 %copy-start.17 = (f32[8]{0:T(128)S(1)}, f32[8]{0:T(128)}, u32[]{:S(2)}) copy-start(f32[8]{0:T(128)} %copy-done.16) | copy-start | bytes 100
  137.6 21.2 %copy-start.19 = (f32[8]{0:T(128)S(1)}, f32[8]{0:T(128)}, u32[]{:S(2)}) copy-start(f32[8]{0:T(128)} %copy-done.18) | copy-start | bytes 100
  137.6 21.2 %copy-start.21 = (f32[8]{0:T(128)S(1)}, f32[8]{0:T(128)}, u32[]{:S(2)}) copy-start(f32[8]{0:T(128)} %get-tuple-element.28) | copy-start | bytes 100
  137.6 21.2 %copy-start.29 = (f32[8]{0:T(128)S(1)}, f32[8]{0:T(128)}, u32[]{:S(2)}) copy-start(f32[8]{0:T(128)} %exp.331) | copy-start | bytes 100
  137.6 21.2 %copy-start.30 = (f32[8]{0:T(128)S(1)}, f32[8]{0:T(128)}, u32[]{:S(2)}) copy-start(f32[8]{0:T(128)} %exp.332) | copy-start | bytes 100
  164.1 55.4 %copy-start.12 = (f32[8]{0:T(128)S(1)}, f32[8]{0:T(128)}, u32[]{:S(2)}) copy-start(f32[8]{0:T(128)} %get-tuple-element.60) | copy-start | bytes 100
  164.1 55.4 %copy-start.14 = (f32[8]{0:T(128)S(1)}, f32[8]{0:T(128)}, u32[]{:S(2)}) copy-start(f32[8]{0:T(128)} %get-tuple-element.62) | copy-start | bytes 100
  166.3 90.5 %all-gather.24.cloned.1.call-start = ((), (), s32[]{:S(2)}) async-start(), calls=%async_computation.3 | async-start | bytes 2621440 | tf_op jit(solution)/shard_map/all_gather | solution.py:26
  222.9 51.1 %all-gather.26.cloned.1.call-start = ((), (), s32[]{:S(2)}) async-start(), calls=%async_computation.4 | async-start | bytes 1572864 | tf_op jit(solution)/shard_map/all_gather | solution.py:26
  259.3 51.7 %all-gather.28.cloned.1.call-start = ((), (), s32[]{:S(2)}) async-start(), calls=%async_computation.5 | async-start | bytes 2621440 | tf_op jit(solution)/shard_map/all_gather | solution.py:26
  292.2 18.9 %copy-start.22 = (f32[8]{0:T(128)S(1)}, f32[8]{0:T(128)}, u32[]{:S(2)}) copy-start(f32[8]{0:T(128)} %get-tuple-element.38) | copy-start | bytes 100
  292.2 18.9 %copy-start.23 = (f32[8]{0:T(128)S(1)}, f32[8]{0:T(128)}, u32[]{:S(2)}) copy-start(f32[8]{0:T(128)} %get-tuple-element.39) | copy-start | bytes 100
  292.2 18.9 %copy-start.24 = (f32[8]{0:T(128)S(1)}, f32[8]{0:T(128)}, u32[]{:S(2)}) copy-start(f32[8]{0:T(128)} %get-tuple-element.40) | copy-start | bytes 100
  (16 other events, 157.2 us)
Sparse Core Ops, SparseCore 0:
  11.6 55.6 all-gather.29
  70.7 33.7 all-gather.17
  107.3 14.4 all-gather.19
  124.0 34.6 all-gather.21
  166.4 53.0 all-gather.31
  223.0 33.7 all-gather.23
  259.5 14.4 all-gather.25
  276.3 34.6 all-gather.27
where the time goes:
time: 327 us; the launch traced here: 325 us
  waiting for transfers between devices  196 us (60%)
  blocking collectives  60.2 us (18%)
  other arithmetic  31 us (9%)
  between operations  15.3 us (5%)
  matrix products  12.2 us (4%)
  local copies, waits for them, and re-layouts  10.4 us (3%)
    all_gather x8, waiting for transfers between devices, prefix_by_axis(): pieces = jax.tree.map(lambda part: lax.all_gather(part, axis), so_far)  196 us
    all_gather x6, blocking collectives, prefix_by_axis(): pieces = jax.tree.map(lambda part: lax.all_gather(part, axis), so_far)  42.3 us
    unnamed x1, blocking collectives  17.9 us
    add x6, other arithmetic, combine(): jnp.exp(latter[0])[:, None, None] * earlier[1] + latter[1]  16.1 us
    unnamed x72, local copies, waits for them, and re-layouts  7.42 us
  transfers between devices with their start and end apart: 8, of which 8 were waited for; matrix products, arithmetic and copies ran while one was open for 5% of the time, Pallas kernels for 0%

commit v1 on v0

v1 whole, which is shorter than its diff:
```python
import math

import jax
import jax.numpy as jnp
from jax import lax
from jax.experimental import pallas as pl
from jax.experimental.pallas import tpu as pltpu
from jax.sharding import Mesh
from jax.sharding import PartitionSpec as P

ALL = ("y", "core", "x", "z")
GROUP = ("x", "z")
EPSILON = 1e-06
HEADS = 8
E = 128
T = 256
PEERS = 32
ROWS = HEADS * E // PEERS
SCALING = 1.0 / math.sqrt(E)
F32 = jnp.float32
BF16 = jnp.bfloat16


def dot(a, b, dims, precision=None):
    return lax.dot_general(a, b, (dims, ((), ())), precision=precision, preferred_element_type=F32)


NN, NT, TN = ((1,), (0,)), ((1,), (1,)), ((0,), (0,))


def lanes(h):
    return slice(h * E, (h + 1) * E)


def causal():
    t = lax.broadcasted_iota(jnp.int32, (T, T), 0)
    s = lax.broadcasted_iota(jnp.int32, (T, T), 1)
    return s <= t


def call(kernel, outs, *args, smem=0, flops=0):
    specs = [pl.BlockSpec(memory_space=pltpu.SMEM)] * smem
    specs += [pl.BlockSpec(memory_space=pltpu.VMEM)] * (len(args) - smem)
    moved = sum(a.size * a.dtype.itemsize for a in args)
    moved += sum(math.prod(s) * jnp.dtype(d).itemsize for s, d in outs)
    return pl.pallas_call(
        kernel,
        out_shape=[jax.ShapeDtypeStruct(s, d) for s, d in outs],
        in_specs=specs,
        out_specs=[pl.BlockSpec(memory_space=pltpu.VMEM)] * len(outs),
        cost_estimate=pl.CostEstimate(flops=flops, bytes_accessed=moved, transcendentals=0),
        compiler_params=pltpu.CompilerParams(vmem_limit_bytes=48 * 1024 * 1024),
    )(*args)


def states_kernel(k_ref, v_ref, decay_ref, sent_ref, run_row_ref, run_col_ref):
    decay = decay_ref[...]
    ones = jnp.where(causal(), 1.0, 0.0).astype(F32)
    run_row = dot(decay, ones, NT, lax.Precision.HIGHEST)
    run_col = dot(ones, decay, NT, lax.Precision.HIGHEST)
    run_row_ref[...] = run_row
    run_col_ref[...] = run_col
    shrink = jnp.exp(run_col[T - 1 : T, :] - run_col)
    totals = jnp.broadcast_to(run_row[:, T - 1 : T], (HEADS, E))
    per_head = E // ROWS
    for h in range(HEADS):
        key_dec = (k_ref[:, lanes(h)].astype(F32) * shrink[:, h : h + 1]).astype(BF16)
        state = dot(key_dec, v_ref[:, lanes(h)], TN)
        for i in range(per_head):
            sent_ref[h * per_head + i, :ROWS, :] = state[i * ROWS : (i + 1) * ROWS]
    for r in range(PEERS):
        sent_ref[r, ROWS:, :] = totals


def local_kernel(q_ref, k_ref, v_ref, run_row_ref, run_col_ref, weights_ref, mixed_ref, query_dec_ref):
    mask = causal()
    growth = jnp.exp(run_col_ref[...])
    for h in range(HEADS):
        q = q_ref[:, lanes(h)]
        gap = run_col_ref[:, h : h + 1] - run_row_ref[h : h + 1, :]
        decay = jnp.exp(jnp.where(mask, gap, -1e30))
        scores = dot(q, k_ref[:, lanes(h)], NT)
        weights = (scores * SCALING * decay).astype(BF16)
        weights_ref[h] = weights
        mixed_ref[:, lanes(h)] = dot(weights, v_ref[:, lanes(h)], NN)
        query_dec_ref[:, lanes(h)] = (q.astype(F32) * growth[:, h : h + 1]).astype(BF16)


def mixed_kernel(mixed_ref, query_dec_ref, g_ref, entering_ref, attended_ref, grad_mixed_ref, state_ref):
    for h in range(HEADS):
        query_dec = query_dec_ref[:, lanes(h)]
        mixed = mixed_ref[:, lanes(h)] + SCALING * dot(query_dec, entering_ref[h].astype(BF16), NN)
        inverse = lax.rsqrt(jnp.mean(mixed * mixed, axis=1, keepdims=True) + EPSILON)
        normed = mixed * inverse
        attended_ref[:, lanes(h)] = normed.astype(BF16)
        g = g_ref[:, lanes(h)].astype(F32)
        grad_mixed = inverse * (g - normed * jnp.mean(g * normed, axis=1, keepdims=True))
        grad_mixed = grad_mixed.astype(BF16)
        grad_mixed_ref[:, lanes(h)] = grad_mixed
        state_ref[h] = SCALING * dot(query_dec, grad_mixed, TN)


def local_grads_kernel(
    q_ref, k_ref, v_ref, run_row_ref, run_col_ref, weights_ref, grad_mixed_ref, entering_ref,
    grad_q_ref, grad_k_ref, grad_v_ref,
):
    mask = causal()
    growth = jnp.exp(run_col_ref[...]) * SCALING
    for h in range(HEADS):
        grad_mixed = grad_mixed_ref[:, lanes(h)]
        gap = run_col_ref[:, h : h + 1] - run_row_ref[h : h + 1, :]
        decay = jnp.exp(jnp.where(mask, gap, -1e30))
        grad_prob = dot(grad_mixed, v_ref[:, lanes(h)], NT)
        grad_score = (grad_prob * SCALING * decay).astype(BF16)
        grad_q = dot(grad_score, k_ref[:, lanes(h)], NN)
        grad_q = grad_q + growth[:, h : h + 1] * dot(grad_mixed, entering_ref[h].astype(BF16), NT)
        grad_q_ref[:, lanes(h)] = grad_q.astype(BF16)
        grad_k_ref[:, lanes(h)] = dot(grad_score, q_ref[:, lanes(h)], TN)
        grad_v_ref[:, lanes(h)] = dot(weights_ref[h], grad_mixed, TN)


def final_kernel(k_ref, v_ref, run_col_ref, part_k_ref, part_v_ref, leaving_ref, grad_k_ref, grad_v_ref):
    run_col = run_col_ref[...]
    shrink = jnp.exp(run_col[T - 1 : T, :] - run_col)
    for h in range(HEADS):
        leaving = leaving_ref[h].astype(BF16)
        column = shrink[:, h : h + 1]
        key_dec = (k_ref[:, lanes(h)].astype(F32) * column).astype(BF16)
        grad_k = part_k_ref[:, lanes(h)] + column * dot(v_ref[:, lanes(h)], leaving, NT)
        grad_v = part_v_ref[:, lanes(h)] + dot(key_dec, leaving, NN)
        grad_k_ref[:, lanes(h)] = grad_k.astype(BF16)
        grad_v_ref[:, lanes(h)] = grad_v.astype(BF16)


def group_total_kernel(place_ref, recv_ref, total_ref, decays_ref):
    head = place_ref[0]
    total = recv_ref[0, :ROWS, :]
    logs = recv_ref[0, pl.ds(ROWS + head, 1), :]
    decays_ref[0:1, :] = jnp.exp(logs)
    for j in range(1, PEERS):
        log = recv_ref[j, pl.ds(ROWS + head, 1), :]
        decay = jnp.exp(log)
        decays_ref[j : j + 1, :] = decay
        total = decay * total + recv_ref[j, :ROWS, :]
        logs = logs + log
    total_ref[:ROWS, :] = total
    total_ref[ROWS:, :] = jnp.broadcast_to(logs, (8, E))


def back_total_kernel(recv_ref, decays_ref, total_ref):
    total = recv_ref[PEERS - 1]
    for j in reversed(range(PEERS - 1)):
        total = decays_ref[j : j + 1, :] * total + recv_ref[j]
    total_ref[...] = total


def spread_kernel(reverse, rows_of, place_ref, recv_ref, decays_ref, far_ref, far_decay_ref, out_ref):
    state = jnp.zeros((ROWS, E), F32)
    for i in range(4):
        counts = place_ref[1 + i] > 0
        stepped = far_decay_ref[i : i + 1, :] * state + far_ref[i, :ROWS, :]
        state = jnp.where(counts, stepped, state)
    for j in reversed(range(PEERS)) if reverse else range(PEERS):
        out_ref[j] = state
        state = decays_ref[j : j + 1, :] * state + recv_ref[j, :ROWS, :]


def shifted(array, by):
    size = 4
    return lax.ppermute(array, "y", [(i, (i + by) % size) for i in range(size)])


def swapped(array):
    return lax.ppermute(array, "core", [(0, 1), (1, 0)])


def exchanged(array):
    return lax.all_to_all(array, GROUP, 0, 0, tiled=True)


def body(q, k, v, log_decay, g):
    y, core = lax.axis_index("y"), lax.axis_index("core")
    head = (lax.axis_index("x") * 8 + lax.axis_index("z")) // (PEERS // HEADS)
    wide = (T, HEADS * E)

    sent, run_row, run_col = call(
        states_kernel, [((PEERS, ROWS + 8, E), F32), ((HEADS, T), F32), ((T, HEADS), F32)],
        k, v, log_decay, flops=2 * HEADS * T * E * E,
    )
    recv = exchanged(sent)
    weights, mixed_part, query_dec = call(
        local_kernel, [((HEADS, T, T), BF16), (wide, F32), (wide, BF16)],
        q, k, v, run_row, run_col, flops=4 * HEADS * T * T * E,
    )
    fold = jnp.stack([head]).astype(jnp.int32)
    total, decays = call(
        group_total_kernel, [((ROWS + 8, E), F32), ((PEERS, E), F32)], fold, recv, smem=1,
    )
    other = swapped(total)
    log_mine, log_other = total[ROWS : ROWS + 1], other[ROWS : ROWS + 1]
    decay_mine, decay_other = jnp.exp(log_mine), jnp.exp(log_other)
    both = jnp.where(core == 0, decay_other * total[:ROWS] + other[:ROWS], decay_mine * other[:ROWS] + total[:ROWS])
    both = jnp.concatenate([both, jnp.broadcast_to(log_mine + log_other, (8, E))])
    near = [shifted(both, by) for by in (3, 2, 1)]
    far = jnp.stack([n[:ROWS] for n in near] + [other[:ROWS]])
    far_decay = jnp.exp(jnp.concatenate([n[ROWS : ROWS + 1] for n in near] + [log_other]))
    flags = [head, y >= 3, y >= 2, y >= 1, core == 1]
    place = jnp.stack([jnp.asarray(f).astype(jnp.int32) for f in flags])
    entering_sent = call(
        lambda *refs: spread_kernel(False, ROWS + 8, *refs), [((PEERS, ROWS, E), F32)],
        place, recv, decays, far, far_decay, smem=1,
    )[0]
    entering = exchanged(entering_sent).reshape(HEADS, E, E)

    attended, grad_mixed, state = call(
        mixed_kernel, [(wide, BF16), (wide, BF16), ((HEADS, E, E), F32)],
        mixed_part, query_dec, g, entering, flops=4 * HEADS * T * E * E,
    )
    recv = exchanged(state.reshape(PEERS, ROWS, E))
    grad_q, part_k, part_v = call(
        local_grads_kernel, [(wide, BF16), (wide, F32), (wide, F32)],
        q, k, v, run_row, run_col, weights, grad_mixed, entering, flops=9 * HEADS * T * T * E,
    )
    total = call(back_total_kernel, [((ROWS, E), F32)], recv, decays)[0]
    other = swapped(total)
    both = jnp.where(core == 0, decay_mine * other + total, decay_other * total + other)
    near = [shifted(both, -by) for by in (3, 2, 1)]
    far = jnp.stack(near + [other])
    far_decay = jnp.stack([far_decay[2], far_decay[1], far_decay[0], far_decay[3]])
    flags = [head, y <= 0, y <= 1, y <= 2, core == 0]
    place = jnp.stack([jnp.asarray(f).astype(jnp.int32) for f in flags])
    leaving_sent = call(
        lambda *refs: spread_kernel(True, ROWS, *refs), [((PEERS, ROWS, E), F32)],
        place, recv, decays, far, far_decay, smem=1,
    )[0]
    leaving = exchanged(leaving_sent).reshape(HEADS, E, E)
    grad_k, grad_v = call(
        final_kernel, [(wide, BF16), (wide, BF16)],
        k, v, run_col, part_k, part_v, leaving, flops=4 * HEADS * T * E * E,
    )
    return attended, grad_q, grad_k, grad_v


def solution(mesh):
    finer = Mesh(mesh.devices.reshape(4, 2, 4, 8), ALL)
    rows = P(ALL, None)
    return jax.shard_map(
        body,
        mesh=finer,
        in_specs=(rows, rows, rows, P(None, ALL), rows),
        out_specs=(rows, rows, rows, rows),
        check_vma=False,
    )
```

time: 327 us -> 131 us (0.40)
  waiting for transfers between devices: 196 us -> 68.2 us
  blocking collectives: 60.2 us -> 0 us
  starting transfers between devices: 0.33 us -> 35.2 us
  other arithmetic: 31 us -> 0.06 us
  between operations: 15.3 us -> 0.88 us
  Pallas kernels: 0 us -> 12.9 us
  matrix products: 12.2 us -> 0 us
    all_gather x8 -> x0, waiting for transfers between devices: 196 us -> none  [prefix_by_axis(): pieces = jax.tree.map(lambda part: lax.all_gather(part, axis), so_far)]
    all_to_all x0 -> x4, waiting for transfers between devices: none -> 59.3 us  [exchanged(): return lax.all_to_all(array, GROUP, 0, 0, tiled=True)]
    all_gather x6 -> x0, blocking collectives: 42.3 us -> none  [prefix_by_axis(): pieces = jax.tree.map(lambda part: lax.all_gather(part, axis), so_far)]
    all_to_all x0 -> x4, starting transfers between devices: none -> 26.2 us  [exchanged(): return lax.all_to_all(array, GROUP, 0, 0, tiled=True)]
    unnamed x1 -> x0, blocking collectives: 17.9 us -> none
    add x8 -> x0, other arithmetic: 16.1 us -> none  [the longest x6 16.1 us: combine(): jnp.exp(latter[0])[:, None, None] * earlier[1] + latter[1]]
    pallas_call x0 -> x9, Pallas kernels: none -> 12.9 us  [call(): pl.pallas_call(kernel, out_shape=[jax.ShapeDtypeStruct(s, d) for s, d in...]
    dot_general x12 -> x0, matrix products: 12.2 us -> none  [the longest x1 2.57 us: body(): jnp.einsum('hts,thf->shf', weights, grad_mixed, preferred_element_type=jn...]
  transfers between devices with their start and end apart: 8 -> 12, of which waited for: 8 -> 11; matrix products, arithmetic and copies ran while one was open for 5% -> 0% of each run, Pallas kernels for 0% -> 3%
where the time goes in v1:
time: 131 us
  waiting for transfers between devices  68.2 us (52%)
  starting transfers between devices  35.2 us (27%)
  local copies, waits for them, and re-layouts  13.4 us (10%)
  Pallas kernels  12.9 us (10%)
    all_to_all x4, waiting for transfers between devices, exchanged(): return lax.all_to_all(array, GROUP, 0, 0, tiled=True)  59.3 us
    all_to_all x4, starting transfers between devices, exchanged(): return lax.all_to_all(array, GROUP, 0, 0, tiled=True)  26.2 us
    unnamed x36, local copies, waits for them, and re-layouts  13.2 us
    pallas_call x9, Pallas kernels, call(): pl.pallas_call(kernel, out_shape=[jax.ShapeDtypeStruct(s, d) for s, d in...  12.9 us
    ppermute x6, starting transfers between devices, shifted(): return lax.ppermute(array, 'y', [(i, (i + by) % size) for i in range(size)])  8.88 us
    ppermute x6, waiting for transfers between devices, shifted(): return lax.ppermute(array, 'y', [(i, (i + by) % size) for i in range(size)])  6.6 us
  transfers between devices with their start and end apart: 12, of which 11 were waited for; matrix products, arithmetic and copies ran while one was open for 0% of the time, Pallas kernels for 3%

profile of v1, /device:TPU:32, one launch (start us, length us, event | category | flops | bytes accessed | tf_op | source)
XLA Modules:
  0.0 130.7 jit_solution(4327803813393355231)
XLA Ops:
  3.4 2.1 %shard_map.84 = (f32[32,40,128]{2,1,0:T(8,128)}, f32[8,256]{1,0:T(8,128)S(1)}, f32[256,8]{1,0:T(8,128)S(1)}) custom-call(bf16[256,1024]{1,0:T(8,128)(2,1)S(1)} %copy-done, bf16[256,1024]{1,0:T(8,128)(2,1)S(1)} %copy-done.2, f32[8,256]{1,0:T(8,128)S(1)} %copy-done.17), custom_call_target="tpu_custom_call" | custom-call | flops 67108864 | bytes 1728512 | tf_op jit(solution)/shard_map/pallas_call | solution.py:46
  5.5 11.2 %all-to-all-start = ((f32[32,40,128]{2,1,0:T(8,128)}), f32[32,40,128]{2,1,0:T(8,128)S(1)}, u32[]{:S(2)}, u32[]{:S(2)}) async-start(f32[32,40,128]{2,1,0:T(8,128)} %get-tuple-element.24), calls=%async_computation | async-start | bytes 1310720 | tf_op jit(solution)/shard_map/all_to_all | solution.py:178
  16.7 20.2 %all-to-all-done.recv_ref.refs_1_ = f32[32,40,128]{2,1,0:T(8,128)S(1)} async-done(((f32[32,40,128]{2,1,0:T(8,128)}), f32[32,40,128]{2,1,0:T(8,128)S(1)}, u32[]{:S(2)}, u32[]{:S(2)}) %all-to-all-start) | async-done | bytes 655392 | tf_op jit(solution)/shard_map/all_to_all | solution.py:178
  38.3 1.7 %collective-permute-start.3 = (f32[40,128]{1,0:T(8,128)S(1)}, f32[40,128]{1,0:T(8,128)S(1)}, u32[]{:S(2)}, u32[]{:S(2)}) collective-permute-start(f32[40,128]{1,0:T(8,128)S(1)} %pad_maximum_fusion.2), channel_id=1, source_target_pairs={{0,64},{64,128},{128,192},{192,0},{1,65},{65,129},{129,193},{193,1... | collective-permute-start | bytes 61448 | tf_op jit(solution)/shard_map/ppermute | solution.py:170
  40.0 2.9 %collective-permute-start.2 = (f32[40,128]{1,0:T(8,128)S(1)}, f32[40,128]{1,0:T(8,128)S(1)}, u32[]{:S(2)}, u32[]{:S(2)}) collective-permute-start(f32[40,128]{1,0:T(8,128)S(1)} %pad_maximum_fusion.2), channel_id=1, source_target_pairs={{0,128},{64,192},{128,0},{192,64},{1,129},{65,193},{129,1},{193,65... | collective-permute-start | bytes 61448 | tf_op jit(solution)/shard_map/ppermute | solution.py:170
  42.9 1.3 %collective-permute-start.1 = (f32[40,128]{1,0:T(8,128)S(1)}, f32[40,128]{1,0:T(8,128)S(1)}, u32[]{:S(2)}, u32[]{:S(2)}) collective-permute-start(f32[40,128]{1,0:T(8,128)S(1)} %pad_maximum_fusion.2), channel_id=1, source_target_pairs={{0,192},{64,0},{128,64},{192,128},{1,193},{65,1},{129,65},{193,129... | collective-permute-start | bytes 61448 | tf_op jit(solution)/shard_map/ppermute | solution.py:170
  45.3 1.4 %collective-permute-done.1 = f32[40,128]{1,0:T(8,128)S(1)} collective-permute-done((f32[40,128]{1,0:T(8,128)S(1)}, f32[40,128]{1,0:T(8,128)S(1)}, u32[]{:S(2)}, u32[]{:S(2)}) %collective-permute-start.1) | collective-permute-done | bytes 20512 | tf_op jit(solution)/shard_map/ppermute | solution.py:170
  46.7 1.4 %shard_map.87 = f32[32,32,128]{2,1,0:T(8,128)} custom-call(s32[5]{0:T(128)S(1)} %stack.101.refs_0_, f32[32,40,128]{2,1,0:T(8,128)S(1)} %all-to-all-done.recv_ref.refs_1_, f32[32,128]{1,0:T(8,128)S(1)} %get-tuple-element.25.refs_2_.decays_ref, f32[4,32,128]{2,1,0:T(8,128)S(1)} %pad_maximum_fusion.refs_3_, f32[4,128]{1,0:T(4,128)S(1)} %maximum_exponential_fusion.refs_4_), custom_call_target="tpu_custom_call" | custom-call | bytes 1263636 | tf_op jit(solution)/shard_map/pallas_call | solution.py:46
  48.2 5.2 %all-to-all-start.1 = ((f32[32,32,128]{2,1,0:T(8,128)}), f32[32,32,128]{2,1,0:T(8,128)S(1)}, u32[]{:S(2)}, u32[]{:S(2)}) async-start(f32[32,32,128]{2,1,0:T(8,128)} %shard_map.87), calls=%async_computation.1 | async-start | bytes 1048576 | tf_op jit(solution)/shard_map/all_to_all | solution.py:178
  56.3 13.5 %all-to-all-done.1 = f32[32,32,128]{2,1,0:T(8,128)S(1)} async-done(((f32[32,32,128]{2,1,0:T(8,128)}), f32[32,32,128]{2,1,0:T(8,128)S(1)}, u32[]{:S(2)}, u32[]{:S(2)}) %all-to-all-start.1) | async-done | bytes 524320 | tf_op jit(solution)/shard_map/all_to_all | solution.py:178
  69.8 1.2 copy-done.6
  71.1 1.9 %shard_map.88 = (bf16[256,1024]{1,0:T(8,128)(2,1)}, bf16[256,1024]{1,0:T(8,128)(2,1)S(1)}, f32[8,128,128]{2,1,0:T(8,128)S(1)}) custom-call(f32[256,1024]{1,0:T(8,128)S(1)} %copy-done.6, bf16[256,1024]{1,0:T(8,128)(2,1)S(1)} %get-tuple-element.23.query_dec_ref, bf16[256,1024]{1,0:T(8,128)(2,1)S(1)} %copy-done.13, f32[8,128,128]{2,1,0:T(8,128)S(1)} %bitcast.30), custom_call_target="tpu_custom_call" | custom-call | flops 134217728 | bytes 4194304 | tf_op jit(solution)/shard_map/pallas_call | solution.py:46
  74.5 4.8 %all-to-all-start.2 = ((f32[32,32,128]{2,1,0:T(8,128)}), f32[32,32,128]{2,1,0:T(8,128)S(1)}, u32[]{:S(2)}, u32[]{:S(2)}) async-start(f32[32,32,128]{2,1,0:T(8,128)} %bitcast.33), calls=%async_computation.2 | async-start | bytes 1048576 | tf_op jit(solution)/shard_map/all_to_all | solution.py:178
  79.5 15.9 %all-to-all-done.2.recv_ref.refs_1_ = f32[32,32,128]{2,1,0:T(8,128)S(1)} async-done(((f32[32,32,128]{2,1,0:T(8,128)}), f32[32,32,128]{2,1,0:T(8,128)S(1)}, u32[]{:S(2)}, u32[]{:S(2)}) %all-to-all-start.2) | async-done | bytes 524320 | tf_op jit(solution)/shard_map/all_to_all | solution.py:178
  96.8 1.6 %collective-permute-start.7 = (f32[32,128]{1,0:T(8,128)S(1)}, f32[32,128]{1,0:T(8,128)S(1)}, u32[]{:S(2)}, u32[]{:S(2)}) collective-permute-start(f32[32,128]{1,0:T(8,128)S(1)} %add_select_fusion), channel_id=1, source_target_pairs={{0,192},{64,0},{128,64},{192,128},{1,193},{65,1},{129,65},{193,129... | collective-permute-start | bytes 49160 | tf_op jit(solution)/shard_map/ppermute | solution.py:170
  100.6 3.0 %collective-permute-done.6 = f32[32,128]{1,0:T(8,128)S(1)} collective-permute-done((f32[32,128]{1,0:T(8,128)S(1)}, f32[32,128]{1,0:T(8,128)S(1)}, u32[]{:S(2)}, u32[]{:S(2)}) %collective-permute-start.6) | collective-permute-done | bytes 16416 | tf_op jit(solution)/shard_map/ppermute | solution.py:170
  104.0 1.4 %shard_map.91 = f32[32,32,128]{2,1,0:T(8,128)} custom-call(s32[5]{0:T(128)S(1)} %stack.115.refs_0_, f32[32,32,128]{2,1,0:T(8,128)S(1)} %all-to-all-done.2.recv_ref.refs_1_, f32[32,128]{1,0:T(8,128)S(1)} %get-tuple-element.25.refs_2_.decays_ref, f32[4,32,128]{2,1,0:T(8,128)S(1)} %pad_maximum_fusion.1.refs_3_, f32[4,128]{1,0:T(4,128)S(1)} %pad_maximum_fusion.3.refs_4_), custom_call_target="tpu_custom_call" | custom-call | bytes 1132564 | tf_op jit(solution)/shard_map/pallas_call | solution.py:46
  105.5 5.0 %all-to-all-start.3 = ((f32[32,32,128]{2,1,0:T(8,128)}), f32[32,32,128]{2,1,0:T(8,128)S(1)}, u32[]{:S(2)}, u32[]{:S(2)}) async-start(f32[32,32,128]{2,1,0:T(8,128)} %shard_map.91), calls=%async_computation.3 | async-start | bytes 1048576 | tf_op jit(solution)/shard_map/all_to_all | solution.py:178
  110.5 1.2 copy-done.8
  111.7 3.5 %shard_map.89 = (bf16[256,1024]{1,0:T(8,128)(2,1)}, f32[256,1024]{1,0:T(8,128)S(1)}, f32[256,1024]{1,0:T(8,128)S(1)}) custom-call(bf16[256,1024]{1,0:T(8,128)(2,1)S(1)} %copy-done.4, bf16[256,1024]{1,0:T(8,128)(2,1)S(1)} %copy-done.1, bf16[256,1024]{1,0:T(8,128)(2,1)S(1)} %copy-done.3, f32[8,256]{1,0:T(8,128)S(1)} %get-tuple-element.20.run_row_ref, ...), custom_call_target="tpu_custom_call" | custom-call | flops 603979776 | bytes 6307840 | tf_op jit(solution)/shard_map/pallas_call | solution.py:46
  117.1 9.6 %all-to-all-done.3 = f32[32,32,128]{2,1,0:T(8,128)S(1)} async-done(((f32[32,32,128]{2,1,0:T(8,128)}), f32[32,32,128]{2,1,0:T(8,128)S(1)}, u32[]{:S(2)}, u32[]{:S(2)}) %all-to-all-start.3) | async-done | bytes 524320 | tf_op jit(solution)/shard_map/all_to_all | solution.py:178
  126.7 1.2 copy-done.10
  127.9 1.2 copy-done.12
  129.2 1.5 %shard_map.92 = (bf16[256,1024]{1,0:T(8,128)(2,1)}, bf16[256,1024]{1,0:T(8,128)(2,1)}) custom-call(bf16[256,1024]{1,0:T(8,128)(2,1)S(1)} %copy-done.1, bf16[256,1024]{1,0:T(8,128)(2,1)S(1)} %copy-done.3, f32[256,8]{1,0:T(8,128)S(1)} %get-tuple-element.21.run_col_ref, f32[256,1024]{1,0:T(8,128)S(1)} %copy-done.10, f32[256,1024]{1,0:T(8,128)S(1)} %copy-done.12, ...), custom_call_target="tpu_custom_call" | custom-call | flops 134217728 | bytes 4726784 | tf_op jit(solution)/shard_map/pallas_call | solution.py:46
  (63 shorter events, 15.8 us)
Async XLA Ops:
  0.6 1.0 copy-start
  1.7 1.0 copy-start.2
  5.5 31.5 %all-to-all-start = ((f32[32,40,128]{2,1,0:T(8,128)}), f32[32,40,128]{2,1,0:T(8,128)S(1)}, u32[]{:S(2)}, u32[]{:S(2)}) async-start(f32[32,40,128]{2,1,0:T(8,128)} %get-tuple-element.24), calls=%async_computation | async-start | bytes 1310720 | tf_op jit(solution)/shard_map/all_to_all | solution.py:178
  37.0 1.3 collective-permute-start
  38.3 6.0 %collective-permute-start.3 = (f32[40,128]{1,0:T(8,128)S(1)}, f32[40,128]{1,0:T(8,128)S(1)}, u32[]{:S(2)}, u32[]{:S(2)}) collective-permute-start(f32[40,128]{1,0:T(8,128)S(1)} %pad_maximum_fusion.2), channel_id=1, source_target_pairs={{0,64},{64,128},{128,192},{192,0},{1,65},{65,129},{129,193},{193,1... | collective-permute-start | bytes 61448 | tf_op jit(solution)/shard_map/ppermute | solution.py:170
  40.0 5.3 %collective-permute-start.2 = (f32[40,128]{1,0:T(8,128)S(1)}, f32[40,128]{1,0:T(8,128)S(1)}, u32[]{:S(2)}, u32[]{:S(2)}) collective-permute-start(f32[40,128]{1,0:T(8,128)S(1)} %pad_maximum_fusion.2), channel_id=1, source_target_pairs={{0,128},{64,192},{128,0},{192,64},{1,129},{65,193},{129,1},{193,65... | collective-permute-start | bytes 61448 | tf_op jit(solution)/shard_map/ppermute | solution.py:170
  42.9 3.8 %collective-permute-start.1 = (f32[40,128]{1,0:T(8,128)S(1)}, f32[40,128]{1,0:T(8,128)S(1)}, u32[]{:S(2)}, u32[]{:S(2)}) collective-permute-start(f32[40,128]{1,0:T(8,128)S(1)} %pad_maximum_fusion.2), channel_id=1, source_target_pairs={{0,192},{64,0},{128,64},{192,128},{1,193},{65,1},{129,65},{193,129... | collective-permute-start | bytes 61448 | tf_op jit(solution)/shard_map/ppermute | solution.py:170
  46.7 6.6 %copy-start.4 = (bf16[256,1024]{1,0:T(8,128)(2,1)S(1)}, bf16[256,1024]{1,0:T(8,128)(2,1)}, u32[]{:S(2)}) copy-start(bf16[256,1024]{1,0:T(8,128)(2,1)} %q_ref.3) | copy-start | bytes 1572868
  48.1 5.2 %copy-start.1 = (bf16[256,1024]{1,0:T(8,128)(2,1)S(1)}, bf16[256,1024]{1,0:T(8,128)(2,1)}, u32[]{:S(2)}) copy-start(bf16[256,1024]{1,0:T(8,128)(2,1)} %k_ref.7) | copy-start | bytes 1572868
  48.2 5.2 %copy-start.3 = (bf16[256,1024]{1,0:T(8,128)(2,1)S(1)}, bf16[256,1024]{1,0:T(8,128)(2,1)}, u32[]{:S(2)}) copy-start(bf16[256,1024]{1,0:T(8,128)(2,1)} %v_ref.7) | copy-start | bytes 1572868
  48.2 21.7 %all-to-all-start.1 = ((f32[32,32,128]{2,1,0:T(8,128)}), f32[32,32,128]{2,1,0:T(8,128)S(1)}, u32[]{:S(2)}, u32[]{:S(2)}) async-start(f32[32,32,128]{2,1,0:T(8,128)} %shard_map.87), calls=%async_computation.1 | async-start | bytes 1048576 | tf_op jit(solution)/shard_map/all_to_all | solution.py:178
  53.3 16.5 %copy-start.13 = (bf16[256,1024]{1,0:T(8,128)(2,1)S(1)}, bf16[256,1024]{1,0:T(8,128)(2,1)}, u32[]{:S(2)}) copy-start(bf16[256,1024]{1,0:T(8,128)(2,1)} %g_ref.1) | copy-start | bytes 1572868
  55.3 1.0 copy-start.7
  69.8 1.2 copy-start.6
  74.5 20.9 %all-to-all-start.2 = ((f32[32,32,128]{2,1,0:T(8,128)}), f32[32,32,128]{2,1,0:T(8,128)S(1)}, u32[]{:S(2)}, u32[]{:S(2)}) async-start(f32[32,32,128]{2,1,0:T(8,128)} %bitcast.33), calls=%async_computation.2 | async-start | bytes 1048576 | tf_op jit(solution)/shard_map/all_to_all | solution.py:178
  95.5 1.3 collective-permute-start.4
  96.8 3.8 %collective-permute-start.7 = (f32[32,128]{1,0:T(8,128)S(1)}, f32[32,128]{1,0:T(8,128)S(1)}, u32[]{:S(2)}, u32[]{:S(2)}) collective-permute-start(f32[32,128]{1,0:T(8,128)S(1)} %add_select_fusion), channel_id=1, source_target_pairs={{0,192},{64,0},{128,64},{192,128},{1,193},{65,1},{129,65},{193,129... | collective-permute-start | bytes 49160 | tf_op jit(solution)/shard_map/ppermute | solution.py:170
  98.3 5.2 %collective-permute-start.6 = (f32[32,128]{1,0:T(8,128)S(1)}, f32[32,128]{1,0:T(8,128)S(1)}, u32[]{:S(2)}, u32[]{:S(2)}) collective-permute-start(f32[32,128]{1,0:T(8,128)S(1)} %add_select_fusion), channel_id=1, source_target_pairs={{0,128},{64,192},{128,0},{192,64},{1,129},{65,193},{129,1},{193,65... | collective-permute-start | bytes 49160 | tf_op jit(solution)/shard_map/ppermute | solution.py:170
  99.1 4.9 %collective-permute-start.5 = (f32[32,128]{1,0:T(8,128)S(1)}, f32[32,128]{1,0:T(8,128)S(1)}, u32[]{:S(2)}, u32[]{:S(2)}) collective-permute-start(f32[32,128]{1,0:T(8,128)S(1)} %add_select_fusion), channel_id=1, source_target_pairs={{0,64},{64,128},{128,192},{192,0},{1,65},{65,129},{129,193},{193,1... | collective-permute-start | bytes 49160 | tf_op jit(solution)/shard_map/ppermute | solution.py:170
  105.5 5.0 %copy-start.16 = (bf16[256,1024]{1,0:T(8,128)(2,1)S(1)}, bf16[256,1024]{1,0:T(8,128)(2,1)}, u32[]{:S(2)}) copy-start(bf16[256,1024]{1,0:T(8,128)(2,1)} %copy-done.15) | copy-start | bytes 1572868
  105.5 21.2 %all-to-all-start.3 = ((f32[32,32,128]{2,1,0:T(8,128)}), f32[32,32,128]{2,1,0:T(8,128)S(1)}, u32[]{:S(2)}, u32[]{:S(2)}) async-start(f32[32,32,128]{2,1,0:T(8,128)} %shard_map.91), calls=%async_computation.3 | async-start | bytes 1048576 | tf_op jit(solution)/shard_map/all_to_all | solution.py:178
  110.5 1.2 copy-start.8
  126.7 1.2 copy-start.10
  127.9 1.2 copy-start.12
  (6 other events, 5.2 us)

commit v2 on v1

v2 whole, which is shorter than its diff:
```python
import math

import jax
import jax.numpy as jnp
from jax import lax
from jax.experimental import pallas as pl
from jax.experimental.pallas import tpu as pltpu
from jax.sharding import Mesh
from jax.sharding import PartitionSpec as P

ALL = ("y", "core", "x", "z")
GROUP = ("x", "z")
EPSILON = 1e-06
HEADS = 8
E = 128
T = 256
PEERS = 32
ROWS = HEADS * E // PEERS
PER_HEAD = PEERS // HEADS
SPAN = ROWS + 1
PIECES = 4
SCALING = 1.0 / math.sqrt(E)
F32 = jnp.float32
BF16 = jnp.bfloat16


def dot(a, b, dims, precision=None):
    return lax.dot_general(a, b, (dims, ((), ())), precision=precision, preferred_element_type=F32)


NN, NT, TN = ((1,), (0,)), ((1,), (1,)), ((0,), (0,))


def lanes(h):
    return slice(h * E, (h + 1) * E)


def causal():
    t = lax.broadcasted_iota(jnp.int32, (T, T), 0)
    s = lax.broadcasted_iota(jnp.int32, (T, T), 1)
    return s <= t


def call(kernel, outs, *args, smem=0, flops=0, hbm_in=(), hbm_out=(), scratch=(), grant=12):
    def spec(space):
        return pl.BlockSpec(memory_space=space)

    ins = [spec(pltpu.SMEM if i < smem else pltpu.HBM if i in hbm_in else pltpu.VMEM) for i in range(len(args))]
    moved = sum(a.size * a.dtype.itemsize for a in args)
    moved += sum(math.prod(s) * jnp.dtype(d).itemsize for s, d in outs)
    return pl.pallas_call(
        kernel,
        out_shape=[pltpu.HBM(s, d) if i in hbm_out else jax.ShapeDtypeStruct(s, d) for i, (s, d) in enumerate(outs)],
        in_specs=ins,
        out_specs=[spec(pltpu.HBM if i in hbm_out else pltpu.VMEM) for i in range(len(outs))],
        scratch_shapes=scratch,
        cost_estimate=pl.CostEstimate(flops=flops, bytes_accessed=moved, transcendentals=0),
        compiler_params=pltpu.CompilerParams(vmem_limit_bytes=grant * 1024 * 1024),
    )(*[pltpu.with_memory_space_constraint(a, pltpu.HBM) if i in hbm_in else a for i, a in enumerate(args)])


def pieces(source, target, sems, count=PIECES):
    size = source.shape[0] // count
    return [
        pltpu.make_async_copy(source.at[pl.ds(i * size, size)], target.at[pl.ds(i * size, size)], sems.at[i])
        for i in range(count)
    ]


def start(copies):
    for copy in copies:
        copy.start()


def wait(copies):
    for copy in copies:
        copy.wait()


def half_copies(pairs, half, wide):
    copies = []
    for source, target, sem in pairs:
        if wide:
            here = pl.ds(half * HEADS * E // 2, HEADS * E // 2)
            copies.append(pltpu.make_async_copy(source.at[:, here], target.at[:, here], sem.at[half]))
        else:
            size = source.shape[0] // 2
            here = pl.ds(half * size, size)
            copies.append(pltpu.make_async_copy(source.at[here], target.at[here], sem.at[half]))
    return copies


def states_kernel(
    k_hbm, v_hbm, decay_hbm, sent_hbm, run_row_hbm, run_col_hbm,
    k_ref, v_ref, decay_ref, sent_ref, run_row_ref, run_col_ref, k_sem, v_sem, out_sem, small_sem,
):
    load_decay = pltpu.make_async_copy(decay_hbm, decay_ref, small_sem.at[0])
    loads = pieces(k_hbm, k_ref, k_sem) + pieces(v_hbm, v_ref, v_sem)
    load_decay.start()
    start(loads)
    ones = jnp.where(causal(), 1.0, 0.0).astype(F32)
    load_decay.wait()
    decay = decay_ref[...]
    run_row = dot(decay, ones, NT, lax.Precision.HIGHEST)
    run_col = dot(ones, decay, NT, lax.Precision.HIGHEST)
    run_row_ref[...] = run_row
    run_col_ref[...] = run_col
    totals = jnp.broadcast_to(run_row[:, T - 1 : T], (HEADS, E))
    small = [
        pltpu.make_async_copy(run_row_ref, run_row_hbm, small_sem.at[1]),
        pltpu.make_async_copy(run_col_ref, run_col_hbm, small_sem.at[2]),
    ]
    start(small)
    shrink = jnp.exp(run_col[T - 1 : T, :] - run_col)
    wait(loads)
    for half in range(2):
        for h in range(half * HEADS // 2, (half + 1) * HEADS // 2):
            key_dec = (k_ref[:, lanes(h)].astype(F32) * shrink[:, h : h + 1]).astype(BF16)
            state = dot(key_dec, v_ref[:, lanes(h)], TN)
            for i in range(PER_HEAD):
                row = (h * PER_HEAD + i) * SPAN
                sent_ref[row : row + ROWS] = state[i * ROWS : (i + 1) * ROWS]
                sent_ref[row + ROWS : row + SPAN] = totals[h : h + 1]
        start(half_copies([(sent_ref, sent_hbm, out_sem)], half, False))
    wait(small)
    for half in range(2):
        wait(half_copies([(sent_ref, sent_hbm, out_sem)], half, False))


def local_kernel(
    q_hbm, k_hbm, v_hbm, run_row_ref, run_col_ref, weights_hbm, mixed_ref, query_dec_ref,
    q_ref, k_ref, v_ref, weights_ref, q_sem, k_sem, v_sem, out_sem,
):
    loads = pieces(q_hbm, q_ref, q_sem) + pieces(k_hbm, k_ref, k_sem) + pieces(v_hbm, v_ref, v_sem)
    start(loads)
    mask = causal()
    growth = jnp.exp(run_col_ref[...])
    wait(loads)
    for h in range(HEADS):
        q = q_ref[:, lanes(h)]
        gap = run_col_ref[:, h : h + 1] - run_row_ref[h : h + 1, :]
        decay = jnp.exp(jnp.where(mask, gap, -1e30))
        scores = dot(q, k_ref[:, lanes(h)], NT)
        weights = (scores * SCALING * decay).astype(BF16)
        weights_ref[h] = weights
        mixed_ref[:, lanes(h)] = dot(weights, v_ref[:, lanes(h)], NN)
        query_dec_ref[:, lanes(h)] = (q.astype(F32) * growth[:, h : h + 1]).astype(BF16)
    stores = pieces(weights_ref, weights_hbm, out_sem)
    start(stores)
    wait(stores)


def mixed_kernel(
    mixed_ref, query_dec_ref, g_ref, entering_ref, attended_hbm, grad_mixed_hbm, state_hbm, half_hbm,
    attended_ref, grad_mixed_ref, state_ref, half_ref, attended_sem, grad_mixed_sem, state_sem, half_sem,
):
    def send(half):
        tall = [(state_ref, state_hbm, state_sem), (half_ref, half_hbm, half_sem)]
        wide = [(attended_ref, attended_hbm, attended_sem), (grad_mixed_ref, grad_mixed_hbm, grad_mixed_sem)]
        return half_copies(tall, half, False) + half_copies(wide, half, True)

    for half in range(2):
        for h in range(half * HEADS // 2, (half + 1) * HEADS // 2):
            query_dec = query_dec_ref[:, lanes(h)]
            entering = entering_ref[h].astype(BF16)
            half_ref[h] = entering
            mixed = mixed_ref[:, lanes(h)] + SCALING * dot(query_dec, entering, NN)
            inverse = lax.rsqrt(jnp.mean(mixed * mixed, axis=1, keepdims=True) + EPSILON)
            normed = mixed * inverse
            attended_ref[:, lanes(h)] = normed.astype(BF16)
            g = g_ref[:, lanes(h)].astype(F32)
            grad_mixed = inverse * (g - normed * jnp.mean(g * normed, axis=1, keepdims=True))
            grad_mixed = grad_mixed.astype(BF16)
            grad_mixed_ref[:, lanes(h)] = grad_mixed
            state_ref[h] = SCALING * dot(query_dec, grad_mixed, TN)
        start(send(half))
    for half in range(2):
        wait(send(half))


def local_grads_kernel(
    q_hbm, k_hbm, v_hbm, weights_hbm, run_row_ref, run_col_ref, grad_mixed_ref, half_ref,
    grad_q_hbm, part_k_ref, part_v_ref,
    q_ref, k_ref, v_ref, weights_ref, grad_q_ref, q_sem, k_sem, v_sem, w_sem, out_sem,
):
    loads = pieces(q_hbm, q_ref, q_sem) + pieces(k_hbm, k_ref, k_sem)
    loads += pieces(v_hbm, v_ref, v_sem) + pieces(weights_hbm, weights_ref, w_sem)
    start(loads)
    mask = causal()
    growth = jnp.exp(run_col_ref[...]) * SCALING
    wait(loads)
    for h in range(HEADS):
        grad_mixed = grad_mixed_ref[:, lanes(h)]
        gap = run_col_ref[:, h : h + 1] - run_row_ref[h : h + 1, :]
        decay = jnp.exp(jnp.where(mask, gap, -1e30))
        grad_prob = dot(grad_mixed, v_ref[:, lanes(h)], NT)
        grad_score = (grad_prob * SCALING * decay).astype(BF16)
        grad_q = dot(grad_score, k_ref[:, lanes(h)], NN)
        grad_q = grad_q + growth[:, h : h + 1] * dot(grad_mixed, half_ref[h], NT)
        grad_q_ref[:, lanes(h)] = grad_q.astype(BF16)
        part_k_ref[:, lanes(h)] = dot(grad_score, q_ref[:, lanes(h)], TN)
        part_v_ref[:, lanes(h)] = dot(weights_ref[h], grad_mixed, TN)
    stores = pieces(grad_q_ref, grad_q_hbm, out_sem)
    start(stores)
    wait(stores)


def final_kernel(
    k_ref, v_ref, run_col_ref, part_k_ref, part_v_hbm, leaving_ref, grad_k_hbm, grad_v_hbm,
    part_v_ref, grad_k_ref, grad_v_ref, in_sem, k_sem, v_sem,
):
    loads = pieces(part_v_hbm, part_v_ref, in_sem)
    start(loads)
    run_col = run_col_ref[...]
    shrink = jnp.exp(run_col[T - 1 : T, :] - run_col)
    for h in range(HEADS):
        grad_k = shrink[:, h : h + 1] * dot(v_ref[:, lanes(h)], leaving_ref[h].astype(BF16), NT)
        grad_k_ref[:, lanes(h)] = (part_k_ref[:, lanes(h)] + grad_k).astype(BF16)
    store_k = pieces(grad_k_ref, grad_k_hbm, k_sem)
    start(store_k)
    wait(loads)
    for h in range(HEADS):
        key_dec = (k_ref[:, lanes(h)].astype(F32) * shrink[:, h : h + 1]).astype(BF16)
        grad_v = dot(key_dec, leaving_ref[h].astype(BF16), NN)
        grad_v_ref[:, lanes(h)] = (part_v_ref[:, lanes(h)] + grad_v).astype(BF16)
    store_v = pieces(grad_v_ref, grad_v_hbm, v_sem)
    start(store_v)
    wait(store_k + store_v)


def group_total_kernel(recv_ref, total_ref, decays_ref):
    total = recv_ref[:ROWS]
    logs = recv_ref[ROWS:SPAN]
    decays_ref[0:1, :] = jnp.exp(logs)
    for j in range(1, PEERS):
        log = recv_ref[j * SPAN + ROWS : (j + 1) * SPAN]
        decay = jnp.exp(log)
        decays_ref[j : j + 1, :] = decay
        total = decay * total + recv_ref[j * SPAN : j * SPAN + ROWS]
        logs = logs + log
    total_ref[:ROWS, :] = total
    total_ref[ROWS:, :] = jnp.broadcast_to(jnp.exp(logs), (8, E))


def back_total_kernel(recv_ref, decays_ref, total_ref):
    total = recv_ref[(PEERS - 1) * ROWS :]
    for j in reversed(range(PEERS - 1)):
        total = decays_ref[j : j + 1, :] * total + recv_ref[j * ROWS : (j + 1) * ROWS]
    total_ref[...] = total


def both_kernel(reverse, place_ref, mine_ref, other_ref, decay_mine_ref, decay_other_ref, both_ref):
    mine, other = mine_ref[:ROWS, :], other_ref[:ROWS, :]
    decay_mine, decay_other = decay_mine_ref[ROWS : ROWS + 1, :], decay_other_ref[ROWS : ROWS + 1, :]
    mine_last = (place_ref[1] == 0) if reverse else (place_ref[1] == 1)
    both = jnp.where(mine_last, decay_mine * other + mine, decay_other * mine + other)
    both_ref[:ROWS, :] = both
    if not reverse:
        both_ref[ROWS:, :] = jnp.broadcast_to(decay_mine * decay_other, (8, E))


def spread_kernel(
    reverse, place_ref, recv_ref, decays_ref, far3_ref, far2_ref, far1_ref, other_ref,
    decay3_ref, decay2_ref, decay1_ref, decay_other_ref, out_ref,
):
    y, core = place_ref[0], place_ref[1]
    span = recv_ref.shape[0] // PEERS
    state = jnp.zeros((ROWS, E), F32)
    steps = [(far3_ref, decay3_ref, 3), (far2_ref, decay2_ref, 2), (far1_ref, decay1_ref, 1)]
    for far_ref, decay_ref, by in steps:
        counts = (y + by < 4) if reverse else (y >= by)
        stepped = decay_ref[ROWS : ROWS + 1, :] * state + far_ref[:ROWS, :]
        state = jnp.where(counts, stepped, state)
    counts = (core == 0) if reverse else (core == 1)
    state = jnp.where(counts, decay_other_ref[ROWS : ROWS + 1, :] * state + other_ref[:ROWS, :], state)
    for j in reversed(range(PEERS)) if reverse else range(PEERS):
        out_ref[j] = state
        state = decays_ref[j : j + 1, :] * state + recv_ref[j * span : j * span + ROWS]


def shifted(array, by):
    return lax.ppermute(array, "y", [(i, (i + by) % 4) for i in range(4)])


def swapped(array):
    return lax.ppermute(array, "core", [(0, 1), (1, 0)])


def exchanged(array):
    return lax.all_to_all(array, GROUP, 0, 0, tiled=True)


def both_of(reverse, rows, place, *args):
    return call(lambda *refs: both_kernel(reverse, *refs), [((rows, E), F32)], place, *args, smem=1)[0]


def spread(reverse, place, *args):
    return call(lambda *refs: spread_kernel(reverse, *refs), [((PEERS, ROWS, E), F32)], place, *args, smem=1)[0]


def body(q, k, v, log_decay, g):
    y, core = lax.axis_index("y"), lax.axis_index("core")
    place = jnp.stack([y, core]).astype(jnp.int32)
    wide = (T, HEADS * E)
    narrow = pltpu.VMEM(wide, BF16)
    square = pltpu.VMEM((HEADS, T, T), BF16)
    sems, two = pltpu.SemaphoreType.DMA((PIECES,)), pltpu.SemaphoreType.DMA((2,))

    sent, run_row, run_col = call(
        states_kernel, [((PEERS * SPAN, E), F32), ((HEADS, T), F32), ((T, HEADS), F32)],
        k, v, log_decay, flops=2 * HEADS * T * E * E, grant=60, hbm_in=(0, 1, 2), hbm_out=(0, 1, 2),
        scratch=[
            narrow, narrow, pltpu.VMEM((HEADS, T), F32), pltpu.VMEM((PEERS * SPAN, E), F32),
            pltpu.VMEM((HEADS, T), F32), pltpu.VMEM((T, HEADS), F32), sems, sems, two, sems,
        ],
    )
    recv = exchanged(sent.reshape(PEERS, 1, SPAN * E)).reshape(PEERS * SPAN, E)
    weights, mixed_part, query_dec = call(
        local_kernel, [((HEADS, T, T), BF16), (wide, F32), (wide, BF16)],
        q, k, v, run_row, run_col, flops=4 * HEADS * T * T * E, grant=60, hbm_in=(0, 1, 2), hbm_out=(0,),
        scratch=[narrow, narrow, narrow, square, sems, sems, sems, sems],
    )
    recv, mixed_part, query_dec = lax.optimization_barrier((recv, mixed_part, query_dec))
    total, decays = call(
        group_total_kernel, [((ROWS + 8, E), F32), ((PEERS, E), F32)], recv,
    )
    other = swapped(total)
    both = both_of(False, ROWS + 8, place, total, other, total, other)
    far3, far2, far1 = [shifted(both, by) for by in (3, 2, 1)]
    entering = exchanged(spread(False, place, recv, decays, far3, far2, far1, other, far3, far2, far1, other))
    entering = entering.reshape(HEADS, E, E)

    attended, grad_mixed, state, half = call(
        mixed_kernel, [(wide, BF16), (wide, BF16), ((HEADS, E, E), F32), ((HEADS, E, E), BF16)],
        mixed_part, query_dec, g, entering, flops=4 * HEADS * T * E * E, hbm_out=(0, 1, 2, 3),
        scratch=[narrow, narrow, pltpu.VMEM((HEADS, E, E), F32), pltpu.VMEM((HEADS, E, E), BF16), two, two, two, two],
    )
    recv = exchanged(state.reshape(PEERS, ROWS, E)).reshape(PEERS * ROWS, E)
    grad_q, part_k, part_v = call(
        local_grads_kernel, [(wide, BF16), (wide, F32), (wide, F32)],
        q, k, v, weights, run_row, run_col, grad_mixed, half, flops=9 * HEADS * T * T * E,
        grant=56, hbm_in=(0, 1, 2, 3), hbm_out=(0,),
        scratch=[narrow, narrow, narrow, square, narrow, sems, sems, sems, sems, sems],
    )
    recv, part_k, part_v = lax.optimization_barrier((recv, part_k, part_v))
    back_total = call(back_total_kernel, [((ROWS, E), F32)], recv, decays)[0]
    back_other = swapped(back_total)
    back_both = both_of(True, ROWS, place, back_total, back_other, total, other)
    back3, back2, back1 = [shifted(back_both, -by) for by in (3, 2, 1)]
    leaving = exchanged(spread(True, place, recv, decays, back3, back2, back1, back_other, far1, far2, far3, other))
    leaving = leaving.reshape(HEADS, E, E)
    grad_k, grad_v = call(
        final_kernel, [(wide, BF16), (wide, BF16)],
        k, v, run_col, part_k, part_v, leaving, flops=4 * HEADS * T * E * E, hbm_in=(4,), hbm_out=(0, 1),
        scratch=[pltpu.VMEM(wide, F32), narrow, narrow, sems, sems, sems],
    )
    return attended, grad_q, grad_k, grad_v


def solution(mesh):
    finer = Mesh(mesh.devices.reshape(4, 2, 4, 8), ALL)
    rows = P(ALL, None)
    return jax.shard_map(
        body,
        mesh=finer,
        in_specs=(rows, rows, rows, P(None, ALL), rows),
        out_specs=(rows, rows, rows, rows),
        check_vma=False,
    )
```

time: 131 us -> 122 us (0.931)
  blocking collectives: 0 us -> 42.4 us
  waiting for transfers between devices: 68.2 us -> 29.5 us
  local copies, waits for them, and re-layouts: 13.4 us -> 0.04 us
  Pallas kernels: 12.9 us -> 23.7 us
  starting transfers between devices: 35.2 us -> 25.2 us
    all_to_all x0 -> x2, blocking collectives: none -> 42.4 us  [exchanged(): return lax.all_to_all(array, GROUP, 0, 0, tiled=True)]
    all_to_all x4 -> x2, waiting for transfers between devices: 59.3 us -> 20.6 us  [exchanged(): return lax.all_to_all(array, GROUP, 0, 0, tiled=True)]
    unnamed x36 -> x14, local copies, waits for them, and re-layouts: 13.2 us -> 0.04 us
    pallas_call x9 -> x11, Pallas kernels: 12.9 us -> 23.7 us  [call(): pl.pallas_call(kernel, out_shape=[pltpu.HBM(s, d) if i in hbm_out else ja...]
    all_to_all x4 -> x2, starting transfers between devices: 26.2 us -> 16.1 us  [exchanged(): return lax.all_to_all(array, GROUP, 0, 0, tiled=True)]
  transfers between devices with their start and end apart: 12 -> 10, of which waited for: 11 -> 9; matrix products, arithmetic and copies ran while one was open for 0% -> 0% of each run, Pallas kernels for 3% -> 11%
where the time goes in v2:
time: 122 us
  blocking collectives  42.4 us (35%)
  waiting for transfers between devices  29.5 us (24%)
  starting transfers between devices  25.2 us (21%)
  Pallas kernels  23.7 us (19%)
    all_to_all x2, blocking collectives, exchanged(): return lax.all_to_all(array, GROUP, 0, 0, tiled=True)  42.4 us
    pallas_call x11, Pallas kernels, call(): pl.pallas_call(kernel, out_shape=[pltpu.HBM(s, d) if i in hbm_out else ja...  23.7 us
    all_to_all x2, waiting for transfers between devices, exchanged(): return lax.all_to_all(array, GROUP, 0, 0, tiled=True)  20.6 us
    all_to_all x2, starting transfers between devices, exchanged(): return lax.all_to_all(array, GROUP, 0, 0, tiled=True)  16.1 us
    ppermute x6, starting transfers between devices, shifted(): return lax.ppermute(array, 'y', [(i, (i + by) % 4) for i in range(4)])  8.96 us
    ppermute x6, waiting for transfers between devices, shifted(): return lax.ppermute(array, 'y', [(i, (i + by) % 4) for i in range(4)])  6.7 us
  transfers between devices with their start and end apart: 10, of which 9 were waited for; matrix products, arithmetic and copies ran while one was open for 0% of the time, Pallas kernels for 11%

profile of v2, /device:TPU:32, one launch (start us, length us, event | category | flops | bytes accessed | tf_op | source)
XLA Modules:
  0.0 121.8 jit_solution(499294034333686358)
XLA Ops:
  0.6 3.3 %shard_map.84 = (f32[1056,128]{1,0:T(8,128)}, f32[8,256]{1,0:T(8,128)}, f32[256,8]{1,0:T(8,128)}) custom-call(bf16[256,1024]{1,0:T(8,128)(2,1)} %k_ref.1, bf16[256,1024]{1,0:T(8,128)(2,1)} %v_ref.1, f32[8,256]{1,0:T(8,128)} %decay_hbm.1), custom_call_target="tpu_custom_call" | custom-call | flops 67108864 | bytes 1613824 | tf_op jit(solution)/shard_map/pallas_call | solution.py:51
  4.0 11.2 %all-to-all-start = ((f32[32,1,4224]{2,1,0:T(1,128)}), f32[32,1,4224]{2,1,0:T(1,128)S(1)}, u32[]{:S(2)}, u32[]{:S(2)}) async-start(f32[32,1,4224]{2,1,0:T(1,128)} %bitcast.14), calls=%async_computation | async-start | bytes 1081344 | tf_op jit(solution)/shard_map/all_to_all | solution.py:290
  15.2 5.5 %shard_map.85 = (bf16[8,256,256]{2,1,0:T(8,128)(2,1)}, f32[256,1024]{1,0:T(8,128)}, bf16[256,1024]{1,0:T(8,128)(2,1)}) custom-call(bf16[256,1024]{1,0:T(8,128)(2,1)} %q_hbm.3, bf16[256,1024]{1,0:T(8,128)(2,1)} %k_ref.1, bf16[256,1024]{1,0:T(8,128)(2,1)} %v_ref.1, f32[8,256]{1,0:T(8,128)} %get-tuple-element.28.run_row_ref, f32[256,8]{1,0:T(8,128)} %get-tuple-element.29.run_col_ref), custom_call_target="tpu_custom_call" | custom-call | flops 268435456 | bytes 4210688 | tf_op jit(solution)/shard_map/pallas_call | solution.py:51
  20.7 12.4 %all-to-all-done = f32[32,1,4224]{2,1,0:T(1,128)S(1)} async-done(((f32[32,1,4224]{2,1,0:T(1,128)}), f32[32,1,4224]{2,1,0:T(1,128)S(1)}, u32[]{:S(2)}, u32[]{:S(2)}) %all-to-all-start) | async-done | bytes 540704 | tf_op jit(solution)/shard_map/all_to_all | solution.py:290
  33.3 1.1 collective-permute-done.refs_2_.refs_4_.refs_6_.refs_10_
  35.0 1.7 %collective-permute-start.3 = (f32[40,128]{1,0:T(8,128)S(1)}, f32[40,128]{1,0:T(8,128)S(1)}, u32[]{:S(2)}, u32[]{:S(2)}) collective-permute-start(f32[40,128]{1,0:T(8,128)S(1)} %shard_map.87), channel_id=1, source_target_pairs={{0,64},{64,128},{128,192},{192,0},{1,65},{65,129},{129,193},{193,1... | collective-permute-start | bytes 61448 | tf_op jit(solution)/shard_map/ppermute | solution.py:282
  36.7 2.9 %collective-permute-start.2 = (f32[40,128]{1,0:T(8,128)S(1)}, f32[40,128]{1,0:T(8,128)S(1)}, u32[]{:S(2)}, u32[]{:S(2)}) collective-permute-start(f32[40,128]{1,0:T(8,128)S(1)} %shard_map.87), channel_id=1, source_target_pairs={{0,128},{64,192},{128,0},{192,64},{1,129},{65,193},{129,1},{193,65... | collective-permute-start | bytes 61448 | tf_op jit(solution)/shard_map/ppermute | solution.py:282
  39.6 1.3 %collective-permute-start.1 = (f32[40,128]{1,0:T(8,128)S(1)}, f32[40,128]{1,0:T(8,128)S(1)}, u32[]{:S(2)}, u32[]{:S(2)}) collective-permute-start(f32[40,128]{1,0:T(8,128)S(1)} %shard_map.87), channel_id=1, source_target_pairs={{0,192},{64,0},{128,64},{192,128},{1,193},{65,1},{129,65},{193,129... | collective-permute-start | bytes 61448 | tf_op jit(solution)/shard_map/ppermute | solution.py:282
  40.9 1.0 collective-permute-done.2.refs_4_.refs_8_
  41.9 1.4 %collective-permute-done.1.refs_3_.refs_7_.refs_9_ = f32[40,128]{1,0:T(8,128)S(1)} collective-permute-done((f32[40,128]{1,0:T(8,128)S(1)}, f32[40,128]{1,0:T(8,128)S(1)}, u32[]{:S(2)}, u32[]{:S(2)}) %collective-permute-start.1) | collective-permute-done | bytes 20512 | tf_op jit(solution)/shard_map/ppermute | solution.py:282
  44.0 21.3 %all_to_all.20 = f32[32,32,128]{2,1,0:T(8,128)S(1)} all-to-all(f32[32,32,128]{2,1,0:T(8,128)S(1)} %shard_map.88), channel_id=1, replica_groups=mesh['y'=4,'core'=2,'x'=4,'z'=8] {'x','z'}, dimensions={0} | all-to-all | bytes 1048576 | tf_op jit(solution)/shard_map/all_to_all | solution.py:290
  65.4 2.2 %shard_map.89 = (bf16[256,1024]{1,0:T(8,128)(2,1)}, bf16[256,1024]{1,0:T(8,128)(2,1)}, f32[8,128,128]{2,1,0:T(8,128)}, bf16[8,128,128]{2,1,0:T(8,128)(2,1)}) custom-call(f32[256,1024]{1,0:T(8,128)S(1)} %copy-done.3, bf16[256,1024]{1,0:T(8,128)(2,1)S(1)} %copy-done.6, bf16[256,1024]{1,0:T(8,128)(2,1)S(1)} %copy-done.5, f32[8,128,128]{2,1,0:T(8,128)S(1)} %bitcast.12), custom_call_target="tpu_custom_call" | custom-call | flops 134217728 | bytes 4456448 | tf_op jit(solution)/shard_map/pallas_call | solution.py:51
  67.5 4.9 %all-to-all-start.2 = ((f32[32,32,128]{2,1,0:T(8,128)}), f32[32,32,128]{2,1,0:T(8,128)S(1)}, u32[]{:S(2)}, u32[]{:S(2)}) async-start(f32[32,32,128]{2,1,0:T(8,128)} %bitcast.15), calls=%async_computation.2 | async-start | bytes 1048576 | tf_op jit(solution)/shard_map/all_to_all | solution.py:290
  72.4 7.9 %shard_map.90 = (bf16[256,1024]{1,0:T(8,128)(2,1)}, f32[256,1024]{1,0:T(8,128)}, f32[256,1024]{1,0:T(8,128)}) custom-call(bf16[256,1024]{1,0:T(8,128)(2,1)} %q_hbm.3, bf16[256,1024]{1,0:T(8,128)(2,1)} %k_ref.1, bf16[256,1024]{1,0:T(8,128)(2,1)} %v_ref.1, bf16[8,256,256]{2,1,0:T(8,128)(2,1)} %get-tuple-element.38.weights_hbm, ...), custom_call_target="tpu_custom_call" | custom-call | flops 603979776 | bytes 6045696 | tf_op jit(solution)/shard_map/pallas_call | solution.py:51
  80.3 8.2 %all-to-all-done.2 = f32[32,32,128]{2,1,0:T(8,128)S(1)} async-done(((f32[32,32,128]{2,1,0:T(8,128)}), f32[32,32,128]{2,1,0:T(8,128)S(1)}, u32[]{:S(2)}, u32[]{:S(2)}) %all-to-all-start.2) | async-done | bytes 524320 | tf_op jit(solution)/shard_map/all_to_all | solution.py:290
  88.6 1.2 collective-permute-done.4.refs_2_.refs_6_
  90.3 1.6 %collective-permute-start.7 = (f32[32,128]{1,0:T(8,128)S(1)}, f32[32,128]{1,0:T(8,128)S(1)}, u32[]{:S(2)}, u32[]{:S(2)}) collective-permute-start(f32[32,128]{1,0:T(8,128)S(1)} %shard_map.92), channel_id=1, source_target_pairs={{0,192},{64,0},{128,64},{192,128},{1,193},{65,1},{129,65},{193,129... | collective-permute-start | bytes 49160 | tf_op jit(solution)/shard_map/ppermute | solution.py:282
  92.0 0.7 collective-permute-start.6
  92.7 0.7 collective-permute-start.5
  93.4 0.8 collective-permute-done.7.refs_5_
  94.2 3.0 %collective-permute-done.6.refs_4_ = f32[32,128]{1,0:T(8,128)S(1)} collective-permute-done((f32[32,128]{1,0:T(8,128)S(1)}, f32[32,128]{1,0:T(8,128)S(1)}, u32[]{:S(2)}, u32[]{:S(2)}) %collective-permute-start.6) | collective-permute-done | bytes 16416 | tf_op jit(solution)/shard_map/ppermute | solution.py:282
  97.7 0.6 shard_map.93
  98.3 21.0 %all_to_all.21 = f32[32,32,128]{2,1,0:T(8,128)S(1)} all-to-all(f32[32,32,128]{2,1,0:T(8,128)S(1)} %shard_map.93), channel_id=1, replica_groups=mesh['y'=4,'core'=2,'x'=4,'z'=8] {'x','z'}, dimensions={0} | all-to-all | bytes 1048576 | tf_op jit(solution)/shard_map/all_to_all | solution.py:290
  119.4 2.4 %shard_map.94 = (bf16[256,1024]{1,0:T(8,128)(2,1)}, bf16[256,1024]{1,0:T(8,128)(2,1)}) custom-call(bf16[256,1024]{1,0:T(8,128)(2,1)S(1)} %copy-done, bf16[256,1024]{1,0:T(8,128)(2,1)S(1)} %copy-done.1, f32[256,8]{1,0:T(8,128)S(1)} %copy-done.2, f32[256,1024]{1,0:T(8,128)S(1)} %copy-done.4, f32[256,1024]{1,0:T(8,128)} %get-tuple-element.46.part_v_hbm, ...), custom_call_target="tpu_custom_call" | custom-call | flops 134217728 | bytes 4726784 | tf_op jit(solution)/shard_map/pallas_call | solution.py:51
  (24 shorter events, 2.6 us)
Async XLA Ops:
  4.0 29.1 %all-to-all-start = ((f32[32,1,4224]{2,1,0:T(1,128)}), f32[32,1,4224]{2,1,0:T(1,128)S(1)}, u32[]{:S(2)}, u32[]{:S(2)}) async-start(f32[32,1,4224]{2,1,0:T(1,128)} %bitcast.14), calls=%async_computation | async-start | bytes 1081344 | tf_op jit(solution)/shard_map/all_to_all | solution.py:290
  33.2 1.3 %collective-permute-start = (f32[40,128]{1,0:T(8,128)S(1)}, f32[40,128]{1,0:T(8,128)S(1)}, u32[]{:S(2)}, u32[]{:S(2)}) collective-permute-start(f32[40,128]{1,0:T(8,128)S(1)} %get-tuple-element.36.refs_1_.refs_3_), channel_id=1, source_target_pairs={{0,32},{32,0},{1,33},{33,1},{2,34},{34,2},{3,35},{35,3},{4,36},{36... | collective-permute-start | bytes 61448 | tf_op jit(solution)/shard_map/ppermute | solution.py:286
  35.0 5.9 %collective-permute-start.3 = (f32[40,128]{1,0:T(8,128)S(1)}, f32[40,128]{1,0:T(8,128)S(1)}, u32[]{:S(2)}, u32[]{:S(2)}) collective-permute-start(f32[40,128]{1,0:T(8,128)S(1)} %shard_map.87), channel_id=1, source_target_pairs={{0,64},{64,128},{128,192},{192,0},{1,65},{65,129},{129,193},{193,1... | collective-permute-start | bytes 61448 | tf_op jit(solution)/shard_map/ppermute | solution.py:282
  36.7 5.3 %collective-permute-start.2 = (f32[40,128]{1,0:T(8,128)S(1)}, f32[40,128]{1,0:T(8,128)S(1)}, u32[]{:S(2)}, u32[]{:S(2)}) collective-permute-start(f32[40,128]{1,0:T(8,128)S(1)} %shard_map.87), channel_id=1, source_target_pairs={{0,128},{64,192},{128,0},{192,64},{1,129},{65,193},{129,1},{193,65... | collective-permute-start | bytes 61448 | tf_op jit(solution)/shard_map/ppermute | solution.py:282
  39.6 3.8 %collective-permute-start.1 = (f32[40,128]{1,0:T(8,128)S(1)}, f32[40,128]{1,0:T(8,128)S(1)}, u32[]{:S(2)}, u32[]{:S(2)}) collective-permute-start(f32[40,128]{1,0:T(8,128)S(1)} %shard_map.87), channel_id=1, source_target_pairs={{0,192},{64,0},{128,64},{192,128},{1,193},{65,1},{129,65},{193,129... | collective-permute-start | bytes 61448 | tf_op jit(solution)/shard_map/ppermute | solution.py:282
  43.3 22.0 %copy-start.3 = (f32[256,1024]{1,0:T(8,128)S(1)}, f32[256,1024]{1,0:T(8,128)}, u32[]{:S(2)}) copy-start(f32[256,1024]{1,0:T(8,128)} %get-tuple-element.32.mixed_ref) | copy-start | bytes 3145732
  44.0 21.4 %copy-start.5 = (bf16[256,1024]{1,0:T(8,128)(2,1)S(1)}, bf16[256,1024]{1,0:T(8,128)(2,1)}, u32[]{:S(2)}) copy-start(bf16[256,1024]{1,0:T(8,128)(2,1)} %g_ref.1) | copy-start | bytes 1572868
  44.0 21.4 %copy-start.6 = (bf16[256,1024]{1,0:T(8,128)(2,1)S(1)}, bf16[256,1024]{1,0:T(8,128)(2,1)}, u32[]{:S(2)}) copy-start(bf16[256,1024]{1,0:T(8,128)(2,1)} %get-tuple-element.33.query_dec_ref) | copy-start | bytes 1572868
  67.5 20.9 %all-to-all-start.2 = ((f32[32,32,128]{2,1,0:T(8,128)}), f32[32,32,128]{2,1,0:T(8,128)S(1)}, u32[]{:S(2)}, u32[]{:S(2)}) async-start(f32[32,32,128]{2,1,0:T(8,128)} %bitcast.15), calls=%async_computation.2 | async-start | bytes 1048576 | tf_op jit(solution)/shard_map/all_to_all | solution.py:290
  88.5 1.3 %collective-permute-start.4 = (f32[32,128]{1,0:T(8,128)S(1)}, f32[32,128]{1,0:T(8,128)S(1)}, u32[]{:S(2)}, u32[]{:S(2)}) collective-permute-start(f32[32,128]{1,0:T(8,128)S(1)} %shard_map.91.refs_1_), channel_id=1, source_target_pairs={{0,32},{32,0},{1,33},{33,1},{2,34},{34,2},{3,35},{35,3},{4,36},{36... | collective-permute-start | bytes 49160 | tf_op jit(solution)/shard_map/ppermute | solution.py:286
  90.3 29.0 %copy-start.4 = (f32[256,1024]{1,0:T(8,128)S(1)}, f32[256,1024]{1,0:T(8,128)}, u32[]{:S(2)}) copy-start(f32[256,1024]{1,0:T(8,128)} %get-tuple-element.45.part_k_ref) | copy-start | bytes 3145732
  90.3 3.9 %collective-permute-start.7 = (f32[32,128]{1,0:T(8,128)S(1)}, f32[32,128]{1,0:T(8,128)S(1)}, u32[]{:S(2)}, u32[]{:S(2)}) collective-permute-start(f32[32,128]{1,0:T(8,128)S(1)} %shard_map.92), channel_id=1, source_target_pairs={{0,192},{64,0},{128,64},{192,128},{1,193},{65,1},{129,65},{193,129... | collective-permute-start | bytes 49160 | tf_op jit(solution)/shard_map/ppermute | solution.py:282
  92.0 5.2 %collective-permute-start.6 = (f32[32,128]{1,0:T(8,128)S(1)}, f32[32,128]{1,0:T(8,128)S(1)}, u32[]{:S(2)}, u32[]{:S(2)}) collective-permute-start(f32[32,128]{1,0:T(8,128)S(1)} %shard_map.92), channel_id=1, source_target_pairs={{0,128},{64,192},{128,0},{192,64},{1,129},{65,193},{129,1},{193,65... | collective-permute-start | bytes 49160 | tf_op jit(solution)/shard_map/ppermute | solution.py:282
  92.7 4.9 %collective-permute-start.5 = (f32[32,128]{1,0:T(8,128)S(1)}, f32[32,128]{1,0:T(8,128)S(1)}, u32[]{:S(2)}, u32[]{:S(2)}) collective-permute-start(f32[32,128]{1,0:T(8,128)S(1)} %shard_map.92), channel_id=1, source_target_pairs={{0,64},{64,128},{128,192},{192,0},{1,65},{65,129},{129,193},{193,1... | collective-permute-start | bytes 49160 | tf_op jit(solution)/shard_map/ppermute | solution.py:282
  97.7 21.7 %copy-start.2 = (f32[256,8]{1,0:T(8,128)S(1)}, f32[256,8]{1,0:T(8,128)}, u32[]{:S(2)}) copy-start(f32[256,8]{1,0:T(8,128)} %get-tuple-element.29.run_col_ref) | copy-start | bytes 24580
  98.3 21.1 %copy-start = (bf16[256,1024]{1,0:T(8,128)(2,1)S(1)}, bf16[256,1024]{1,0:T(8,128)(2,1)}, u32[]{:S(2)}) copy-start(bf16[256,1024]{1,0:T(8,128)(2,1)} %k_ref.1) | copy-start | bytes 1572868
  98.3 21.1 %copy-start.1 = (bf16[256,1024]{1,0:T(8,128)(2,1)S(1)}, bf16[256,1024]{1,0:T(8,128)(2,1)}, u32[]{:S(2)}) copy-start(bf16[256,1024]{1,0:T(8,128)(2,1)} %v_ref.1) | copy-start | bytes 1572868

commit v3 on v2

--- a/solution.py
+++ b/solution.py
@@ -41,7 +41,7 @@
     return s <= t
 
 
-def call(kernel, outs, *args, smem=0, flops=0, hbm_in=(), hbm_out=(), scratch=(), grant=12):
+def call(kernel, outs, *args, smem=0, flops=0, hbm_in=(), hbm_out=(), scratch=(), grant=16):
     def spec(space):
         return pl.BlockSpec(memory_space=space)
 
@@ -249,10 +249,11 @@
     total_ref[...] = total
 
 
-def both_kernel(reverse, place_ref, mine_ref, other_ref, decay_mine_ref, decay_other_ref, both_ref):
+def both_kernel(reverse, mine_ref, other_ref, decay_mine_ref, decay_other_ref, both_ref):
     mine, other = mine_ref[:ROWS, :], other_ref[:ROWS, :]
     decay_mine, decay_other = decay_mine_ref[ROWS : ROWS + 1, :], decay_other_ref[ROWS : ROWS + 1, :]
-    mine_last = (place_ref[1] == 0) if reverse else (place_ref[1] == 1)
+    core = lax.axis_index("core")
+    mine_last = (core == 0) if reverse else (core == 1)
     both = jnp.where(mine_last, decay_mine * other + mine, decay_other * mine + other)
     both_ref[:ROWS, :] = both
     if not reverse:
@@ -260,10 +261,10 @@
 
 
 def spread_kernel(
-    reverse, place_ref, recv_ref, decays_ref, far3_ref, far2_ref, far1_ref, other_ref,
+    reverse, recv_ref, decays_ref, far3_ref, far2_ref, far1_ref, other_ref,
     decay3_ref, decay2_ref, decay1_ref, decay_other_ref, out_ref,
 ):
-    y, core = place_ref[0], place_ref[1]
+    y, core = lax.axis_index("y"), lax.axis_index("core")
     span = recv_ref.shape[0] // PEERS
     state = jnp.zeros((ROWS, E), F32)
     steps = [(far3_ref, decay3_ref, 3), (far2_ref, decay2_ref, 2), (far1_ref, decay1_ref, 1)]
@@ -290,17 +291,15 @@
     return lax.all_to_all(array, GROUP, 0, 0, tiled=True)
 
 
-def both_of(reverse, rows, place, *args):
-    return call(lambda *refs: both_kernel(reverse, *refs), [((rows, E), F32)], place, *args, smem=1)[0]
-
-
-def spread(reverse, place, *args):
-    return call(lambda *refs: spread_kernel(reverse, *refs), [((PEERS, ROWS, E), F32)], place, *args, smem=1)[0]
+def both_of(reverse, rows, *args):
+    return call(lambda *refs: both_kernel(reverse, *refs), [((rows, E), F32)], *args)[0]
+
+
+def spread(reverse, *args):
+    return call(lambda *refs: spread_kernel(reverse, *refs), [((PEERS, ROWS, E), F32)], *args)[0]
 
 
 def body(q, k, v, log_decay, g):
-    y, core = lax.axis_index("y"), lax.axis_index("core")
-    place = jnp.stack([y, core]).astype(jnp.int32)
     wide = (T, HEADS * E)
     narrow = pltpu.VMEM(wide, BF16)
     square = pltpu.VMEM((HEADS, T, T), BF16)
@@ -308,7 +307,7 @@
 
     sent, run_row, run_col = call(
         states_kernel, [((PEERS * SPAN, E), F32), ((HEADS, T), F32), ((T, HEADS), F32)],
-        k, v, log_decay, flops=2 * HEADS * T * E * E, grant=60, hbm_in=(0, 1, 2), hbm_out=(0, 1, 2),
+        k, v, log_decay, flops=2 * HEADS * T * E * E, hbm_in=(0, 1, 2), hbm_out=(0, 1, 2),
         scratch=[
             narrow, narrow, pltpu.VMEM((HEADS, T), F32), pltpu.VMEM((PEERS * SPAN, E), F32),
             pltpu.VMEM((HEADS, T), F32), pltpu.VMEM((T, HEADS), F32), sems, sems, two, sems,
@@ -317,7 +316,7 @@
     recv = exchanged(sent.reshape(PEERS, 1, SPAN * E)).reshape(PEERS * SPAN, E)
     weights, mixed_part, query_dec = call(
         local_kernel, [((HEADS, T, T), BF16), (wide, F32), (wide, BF16)],
-        q, k, v, run_row, run_col, flops=4 * HEADS * T * T * E, grant=60, hbm_in=(0, 1, 2), hbm_out=(0,),
+        q, k, v, run_row, run_col, flops=4 * HEADS * T * T * E, hbm_in=(0, 1, 2), hbm_out=(0,),
         scratch=[narrow, narrow, narrow, square, sems, sems, sems, sems],
     )
     recv, mixed_part, query_dec = lax.optimization_barrier((recv, mixed_part, query_dec))
@@ -325,9 +324,9 @@
         group_total_kernel, [((ROWS + 8, E), F32), ((PEERS, E), F32)], recv,
     )
     other = swapped(total)
-    both = both_of(False, ROWS + 8, place, total, other, total, other)
+    both = both_of(False, ROWS + 8, total, other, total, other)
     far3, far2, far1 = [shifted(both, by) for by in (3, 2, 1)]
-    entering = exchanged(spread(False, place, recv, decays, far3, far2, far1, other, far3, far2, far1, other))
+    entering = exchanged(spread(False, recv, decays, far3, far2, far1, other, far3, far2, far1, other))
     entering = entering.reshape(HEADS, E, E)
 
     attended, grad_mixed, state, half = call(
@@ -339,15 +338,15 @@
     grad_q, part_k, part_v = call(
         local_grads_kernel, [(wide, BF16), (wide, F32), (wide, F32)],
         q, k, v, weights, run_row, run_col, grad_mixed, half, flops=9 * HEADS * T * T * E,
-        grant=56, hbm_in=(0, 1, 2, 3), hbm_out=(0,),
+        hbm_in=(0, 1, 2, 3), hbm_out=(0,),
         scratch=[narrow, narrow, narrow, square, narrow, sems, sems, sems, sems, sems],
     )
     recv, part_k, part_v = lax.optimization_barrier((recv, part_k, part_v))
     back_total = call(back_total_kernel, [((ROWS, E), F32)], recv, decays)[0]
     back_other = swapped(back_total)
-    back_both = both_of(True, ROWS, place, back_total, back_other, total, other)
+    back_both = both_of(True, ROWS, back_total, back_other, total, other)
     back3, back2, back1 = [shifted(back_both, -by) for by in (3, 2, 1)]
-    leaving = exchanged(spread(True, place, recv, decays, back3, back2, back1, back_other, far1, far2, far3, other))
+    leaving = exchanged(spread(True, recv, decays, back3, back2, back1, back_other, far1, far2, far3, other))
     leaving = leaving.reshape(HEADS, E, E)
     grad_k, grad_v = call(
         final_kernel, [(wide, BF16), (wide, BF16)],

time: 122 us -> 120 us (0.984)
  Pallas kernels: 23.7 us -> 17.1 us
  waiting for transfers between devices: 29.5 us -> 33.1 us
    pallas_call x11, Pallas kernels: 23.7 us -> 17.1 us  [call(): pl.pallas_call(kernel, out_shape=[pltpu.HBM(s, d) if i in hbm_out else ja...]
    all_to_all x2, waiting for transfers between devices: 20.6 us -> 24 us  [exchanged(): return lax.all_to_all(array, GROUP, 0, 0, tiled=True)]
  transfers between devices with their start and end apart: 10 -> 10, of which waited for: 9 -> 9; matrix products, arithmetic and copies ran while one was open for 0% -> 0% of each run, Pallas kernels for 11% -> 7%
where the time goes in v3:
time: 120 us
  blocking collectives  42.4 us (35%)
  waiting for transfers between devices  33.1 us (28%)
  starting transfers between devices  25.4 us (21%)
  Pallas kernels  17.1 us (14%)
    all_to_all x2, blocking collectives, exchanged(): return lax.all_to_all(array, GROUP, 0, 0, tiled=True)  42.4 us
    all_to_all x2, waiting for transfers between devices, exchanged(): return lax.all_to_all(array, GROUP, 0, 0, tiled=True)  24 us
    pallas_call x11, Pallas kernels, call(): pl.pallas_call(kernel, out_shape=[pltpu.HBM(s, d) if i in hbm_out else ja...  17.1 us
    all_to_all x2, starting transfers between devices, exchanged(): return lax.all_to_all(array, GROUP, 0, 0, tiled=True)  16.3 us
    ppermute x6, starting transfers between devices, shifted(): return lax.ppermute(array, 'y', [(i, (i + by) % 4) for i in range(4)])  8.94 us
    ppermute x6, waiting for transfers between devices, shifted(): return lax.ppermute(array, 'y', [(i, (i + by) % 4) for i in range(4)])  6.7 us
  transfers between devices with their start and end apart: 10, of which 9 were waited for; matrix products, arithmetic and copies ran while one was open for 0% of the time, Pallas kernels for 7%

profile of v3, /device:TPU:32, one launch (start us, length us, event | category | flops | bytes accessed | tf_op | source)
XLA Modules:
  0.0 119.8 jit_solution(2142095565222151999)
XLA Ops:
  0.6 3.3 %shard_map.84 = (f32[1056,128]{1,0:T(8,128)}, f32[8,256]{1,0:T(8,128)}, f32[256,8]{1,0:T(8,128)}) custom-call(bf16[256,1024]{1,0:T(8,128)(2,1)} %k_ref.1, bf16[256,1024]{1,0:T(8,128)(2,1)} %v_ref.1, f32[8,256]{1,0:T(8,128)} %decay_hbm.1), custom_call_target="tpu_custom_call" | custom-call | flops 67108864 | bytes 1613824 | tf_op jit(solution)/shard_map/pallas_call | solution.py:51
  4.0 11.3 %all-to-all-start = ((f32[32,1,4224]{2,1,0:T(1,128)}), f32[32,1,4224]{2,1,0:T(1,128)S(1)}, u32[]{:S(2)}, u32[]{:S(2)}) async-start(f32[32,1,4224]{2,1,0:T(1,128)} %bitcast.12), calls=%async_computation | async-start | bytes 1081344 | tf_op jit(solution)/shard_map/all_to_all | solution.py:291
  15.3 3.4 %shard_map.85 = (bf16[8,256,256]{2,1,0:T(8,128)(2,1)}, f32[256,1024]{1,0:T(8,128)S(1)}, bf16[256,1024]{1,0:T(8,128)(2,1)S(1)}) custom-call(bf16[256,1024]{1,0:T(8,128)(2,1)} %q_hbm.3, bf16[256,1024]{1,0:T(8,128)(2,1)} %k_ref.1, bf16[256,1024]{1,0:T(8,128)(2,1)} %v_ref.1, f32[8,256]{1,0:T(8,128)S(1)} %copy-done.7, f32[256,8]{1,0:T(8,128)S(1)} %copy-done.2), custom_call_target="tpu_custom_call" | custom-call | flops 268435456 | bytes 4210688 | tf_op jit(solution)/shard_map/pallas_call | solution.py:51
  18.8 14.5 %all-to-all-done = f32[32,1,4224]{2,1,0:T(1,128)S(1)} async-done(((f32[32,1,4224]{2,1,0:T(1,128)}), f32[32,1,4224]{2,1,0:T(1,128)S(1)}, u32[]{:S(2)}, u32[]{:S(2)}) %all-to-all-start) | async-done | bytes 540704 | tf_op jit(solution)/shard_map/all_to_all | solution.py:291
  33.4 1.2 collective-permute-done.refs_1_.refs_3_.refs_5_.refs_9_
  34.6 1.7 %collective-permute-start.3 = (f32[40,128]{1,0:T(8,128)S(1)}, f32[40,128]{1,0:T(8,128)S(1)}, u32[]{:S(2)}, u32[]{:S(2)}) collective-permute-start(f32[40,128]{1,0:T(8,128)S(1)} %shard_map.87), channel_id=1, source_target_pairs={{0,64},{64,128},{128,192},{192,0},{1,65},{65,129},{129,193},{193,1... | collective-permute-start | bytes 61448 | tf_op jit(solution)/shard_map/ppermute | solution.py:283
  36.3 2.9 %collective-permute-start.2 = (f32[40,128]{1,0:T(8,128)S(1)}, f32[40,128]{1,0:T(8,128)S(1)}, u32[]{:S(2)}, u32[]{:S(2)}) collective-permute-start(f32[40,128]{1,0:T(8,128)S(1)} %shard_map.87), channel_id=1, source_target_pairs={{0,128},{64,192},{128,0},{192,64},{1,129},{65,193},{129,1},{193,65... | collective-permute-start | bytes 61448 | tf_op jit(solution)/shard_map/ppermute | solution.py:283
  39.2 1.3 %collective-permute-start.1 = (f32[40,128]{1,0:T(8,128)S(1)}, f32[40,128]{1,0:T(8,128)S(1)}, u32[]{:S(2)}, u32[]{:S(2)}) collective-permute-start(f32[40,128]{1,0:T(8,128)S(1)} %shard_map.87), channel_id=1, source_target_pairs={{0,192},{64,0},{128,64},{192,128},{1,193},{65,1},{129,65},{193,129... | collective-permute-start | bytes 61448 | tf_op jit(solution)/shard_map/ppermute | solution.py:283
  40.5 1.0 collective-permute-done.2.refs_3_.refs_7_
  41.6 1.4 %collective-permute-done.1.refs_2_.refs_6_.refs_8_ = f32[40,128]{1,0:T(8,128)S(1)} collective-permute-done((f32[40,128]{1,0:T(8,128)S(1)}, f32[40,128]{1,0:T(8,128)S(1)}, u32[]{:S(2)}, u32[]{:S(2)}) %collective-permute-start.1) | collective-permute-done | bytes 20512 | tf_op jit(solution)/shard_map/ppermute | solution.py:283
  43.0 21.3 %all_to_all.20 = f32[32,32,128]{2,1,0:T(8,128)S(1)} all-to-all(f32[32,32,128]{2,1,0:T(8,128)S(1)} %shard_map.88), channel_id=1, replica_groups=mesh['y'=4,'core'=2,'x'=4,'z'=8] {'x','z'}, dimensions={0} | all-to-all | bytes 1048576 | tf_op jit(solution)/shard_map/all_to_all | solution.py:291
  64.4 2.2 %shard_map.89 = (bf16[256,1024]{1,0:T(8,128)(2,1)}, bf16[256,1024]{1,0:T(8,128)(2,1)}, f32[8,128,128]{2,1,0:T(8,128)}, bf16[8,128,128]{2,1,0:T(8,128)(2,1)}) custom-call(f32[256,1024]{1,0:T(8,128)S(1)} %get-tuple-element.32.mixed_ref, bf16[256,1024]{1,0:T(8,128)(2,1)S(1)} %get-tuple-element.33.query_dec_ref, bf16[256,1024]{1,0:T(8,128)(2,1)S(1)} %copy-done.4, ...), custom_call_target="tpu_custom_call" | custom-call | flops 134217728 | bytes 4456448 | tf_op jit(solution)/shard_map/pallas_call | solution.py:51
  66.6 5.0 %all-to-all-start.2 = ((f32[32,32,128]{2,1,0:T(8,128)}), f32[32,32,128]{2,1,0:T(8,128)S(1)}, u32[]{:S(2)}, u32[]{:S(2)}) async-start(f32[32,32,128]{2,1,0:T(8,128)} %bitcast.13), calls=%async_computation.2 | async-start | bytes 1048576 | tf_op jit(solution)/shard_map/all_to_all | solution.py:291
  71.6 5.4 %shard_map.90 = (bf16[256,1024]{1,0:T(8,128)(2,1)}, f32[256,1024]{1,0:T(8,128)S(1)}, f32[256,1024]{1,0:T(8,128)S(1)}) custom-call(bf16[256,1024]{1,0:T(8,128)(2,1)} %q_hbm.3, bf16[256,1024]{1,0:T(8,128)(2,1)} %k_ref.1, bf16[256,1024]{1,0:T(8,128)(2,1)} %v_ref.1, bf16[8,256,256]{2,1,0:T(8,128)(2,1)} %get-tuple-element.38.weights_hbm, f32[8,256]{1,0:T(8,128)S(1)} %copy-done.7, ...), custom_call_target="tpu_custom_call" | custom-call | flops 603979776 | bytes 6045696 | tf_op jit(solution)/shard_map/pallas_call | solution.py:51
  77.0 1.0 copy-done.3
  78.0 9.6 %all-to-all-done.2 = f32[32,32,128]{2,1,0:T(8,128)S(1)} async-done(((f32[32,32,128]{2,1,0:T(8,128)}), f32[32,32,128]{2,1,0:T(8,128)S(1)}, u32[]{:S(2)}, u32[]{:S(2)}) %all-to-all-start.2) | async-done | bytes 524320 | tf_op jit(solution)/shard_map/all_to_all | solution.py:291
  87.8 1.2 collective-permute-done.4.refs_1_.refs_5_
  89.0 1.6 %collective-permute-start.7 = (f32[32,128]{1,0:T(8,128)S(1)}, f32[32,128]{1,0:T(8,128)S(1)}, u32[]{:S(2)}, u32[]{:S(2)}) collective-permute-start(f32[32,128]{1,0:T(8,128)S(1)} %shard_map.92), channel_id=1, source_target_pairs={{0,192},{64,0},{128,64},{192,128},{1,193},{65,1},{129,65},{193,129... | collective-permute-start | bytes 49160 | tf_op jit(solution)/shard_map/ppermute | solution.py:283
  90.6 0.7 collective-permute-start.6
  91.3 0.7 collective-permute-start.5
  92.0 0.8 collective-permute-done.7.refs_4_
  92.8 3.1 %collective-permute-done.6.refs_3_ = f32[32,128]{1,0:T(8,128)S(1)} collective-permute-done((f32[32,128]{1,0:T(8,128)S(1)}, f32[32,128]{1,0:T(8,128)S(1)}, u32[]{:S(2)}, u32[]{:S(2)}) %collective-permute-start.6) | collective-permute-done | bytes 16416 | tf_op jit(solution)/shard_map/ppermute | solution.py:283
  96.4 21.0 %all_to_all.21 = f32[32,32,128]{2,1,0:T(8,128)S(1)} all-to-all(f32[32,32,128]{2,1,0:T(8,128)S(1)} %shard_map.93), channel_id=1, replica_groups=mesh['y'=4,'core'=2,'x'=4,'z'=8] {'x','z'}, dimensions={0} | all-to-all | bytes 1048576 | tf_op jit(solution)/shard_map/all_to_all | solution.py:291
  117.4 2.4 %shard_map.94 = (bf16[256,1024]{1,0:T(8,128)(2,1)}, bf16[256,1024]{1,0:T(8,128)(2,1)}) custom-call(bf16[256,1024]{1,0:T(8,128)(2,1)S(1)} %copy-done, bf16[256,1024]{1,0:T(8,128)(2,1)S(1)} %copy-done.1, f32[256,8]{1,0:T(8,128)S(1)} %copy-done.2, f32[256,1024]{1,0:T(8,128)S(1)} %get-tuple-element.45.part_k_ref, f32[256,1024]{1,0:T(8,128)} %copy-done.3, ...), custom_call_target="tpu_custom_call" | custom-call | flops 134217728 | bytes 4726784 | tf_op jit(solution)/shard_map/pallas_call | solution.py:51
  (25 shorter events, 1.0 us)
Async XLA Ops:
  4.0 11.4 %copy-start.2 = (f32[256,8]{1,0:T(8,128)S(1)}, f32[256,8]{1,0:T(8,128)}, u32[]{:S(2)}) copy-start(f32[256,8]{1,0:T(8,128)} %get-tuple-element.29.run_col_ref) | copy-start | bytes 24580
  4.0 11.4 %copy-start.7 = (f32[8,256]{1,0:T(8,128)S(1)}, f32[8,256]{1,0:T(8,128)}, u32[]{:S(2)}) copy-start(f32[8,256]{1,0:T(8,128)} %get-tuple-element.28.run_row_ref) | copy-start | bytes 24580
  4.0 29.3 %all-to-all-start = ((f32[32,1,4224]{2,1,0:T(1,128)}), f32[32,1,4224]{2,1,0:T(1,128)S(1)}, u32[]{:S(2)}, u32[]{:S(2)}) async-start(f32[32,1,4224]{2,1,0:T(1,128)} %bitcast.12), calls=%async_computation | async-start | bytes 1081344 | tf_op jit(solution)/shard_map/all_to_all | solution.py:291
  33.3 1.3 %collective-permute-start = (f32[40,128]{1,0:T(8,128)S(1)}, f32[40,128]{1,0:T(8,128)S(1)}, u32[]{:S(2)}, u32[]{:S(2)}) collective-permute-start(f32[40,128]{1,0:T(8,128)S(1)} %get-tuple-element.36.refs_0_.refs_2_), channel_id=1, source_target_pairs={{0,32},{32,0},{1,33},{33,1},{2,34},{34,2},{3,35},{35,3},{4,36},{36... | collective-permute-start | bytes 61448 | tf_op jit(solution)/shard_map/ppermute | solution.py:287
  34.6 5.9 %collective-permute-start.3 = (f32[40,128]{1,0:T(8,128)S(1)}, f32[40,128]{1,0:T(8,128)S(1)}, u32[]{:S(2)}, u32[]{:S(2)}) collective-permute-start(f32[40,128]{1,0:T(8,128)S(1)} %shard_map.87), channel_id=1, source_target_pairs={{0,64},{64,128},{128,192},{192,0},{1,65},{65,129},{129,193},{193,1... | collective-permute-start | bytes 61448 | tf_op jit(solution)/shard_map/ppermute | solution.py:283
  36.3 5.3 %collective-permute-start.2 = (f32[40,128]{1,0:T(8,128)S(1)}, f32[40,128]{1,0:T(8,128)S(1)}, u32[]{:S(2)}, u32[]{:S(2)}) collective-permute-start(f32[40,128]{1,0:T(8,128)S(1)} %shard_map.87), channel_id=1, source_target_pairs={{0,128},{64,192},{128,0},{192,64},{1,129},{65,193},{129,1},{193,65... | collective-permute-start | bytes 61448 | tf_op jit(solution)/shard_map/ppermute | solution.py:283
  39.2 3.8 %collective-permute-start.1 = (f32[40,128]{1,0:T(8,128)S(1)}, f32[40,128]{1,0:T(8,128)S(1)}, u32[]{:S(2)}, u32[]{:S(2)}) collective-permute-start(f32[40,128]{1,0:T(8,128)S(1)} %shard_map.87), channel_id=1, source_target_pairs={{0,192},{64,0},{128,64},{192,128},{1,193},{65,1},{129,65},{193,129... | collective-permute-start | bytes 61448 | tf_op jit(solution)/shard_map/ppermute | solution.py:283
  43.0 21.4 %copy-start.4 = (bf16[256,1024]{1,0:T(8,128)(2,1)S(1)}, bf16[256,1024]{1,0:T(8,128)(2,1)}, u32[]{:S(2)}) copy-start(bf16[256,1024]{1,0:T(8,128)(2,1)} %g_ref.1) | copy-start | bytes 1572868
  66.6 5.0 %copy-start.5 = (bf16[256,1024]{1,0:T(8,128)(2,1)S(1)}, bf16[256,1024]{1,0:T(8,128)(2,1)}, u32[]{:S(2)}) copy-start(bf16[256,1024]{1,0:T(8,128)(2,1)} %get-tuple-element.39.grad_mixed_ref) | copy-start | bytes 1572868
  66.6 5.0 %copy-start.6 = (bf16[8,128,128]{2,1,0:T(8,128)(2,1)S(1)}, bf16[8,128,128]{2,1,0:T(8,128)(2,1)}, u32[]{:S(2)}) copy-start(bf16[8,128,128]{2,1,0:T(8,128)(2,1)} %get-tuple-element.40.half_ref) | copy-start | bytes 786436
  66.6 21.0 %all-to-all-start.2 = ((f32[32,32,128]{2,1,0:T(8,128)}), f32[32,32,128]{2,1,0:T(8,128)S(1)}, u32[]{:S(2)}, u32[]{:S(2)}) async-start(f32[32,32,128]{2,1,0:T(8,128)} %bitcast.13), calls=%async_computation.2 | async-start | bytes 1048576 | tf_op jit(solution)/shard_map/all_to_all | solution.py:291
  77.0 1.0 copy-start.3
  87.7 1.3 %collective-permute-start.4 = (f32[32,128]{1,0:T(8,128)S(1)}, f32[32,128]{1,0:T(8,128)S(1)}, u32[]{:S(2)}, u32[]{:S(2)}) collective-permute-start(f32[32,128]{1,0:T(8,128)S(1)} %shard_map.91.refs_0_), channel_id=1, source_target_pairs={{0,32},{32,0},{1,33},{33,1},{2,34},{34,2},{3,35},{35,3},{4,36},{36... | collective-permute-start | bytes 49160 | tf_op jit(solution)/shard_map/ppermute | solution.py:287
  89.0 3.8 %collective-permute-start.7 = (f32[32,128]{1,0:T(8,128)S(1)}, f32[32,128]{1,0:T(8,128)S(1)}, u32[]{:S(2)}, u32[]{:S(2)}) collective-permute-start(f32[32,128]{1,0:T(8,128)S(1)} %shard_map.92), channel_id=1, source_target_pairs={{0,192},{64,0},{128,64},{192,128},{1,193},{65,1},{129,65},{193,129... | collective-permute-start | bytes 49160 | tf_op jit(solution)/shard_map/ppermute | solution.py:283
  90.6 5.2 %collective-permute-start.6 = (f32[32,128]{1,0:T(8,128)S(1)}, f32[32,128]{1,0:T(8,128)S(1)}, u32[]{:S(2)}, u32[]{:S(2)}) collective-permute-start(f32[32,128]{1,0:T(8,128)S(1)} %shard_map.92), channel_id=1, source_target_pairs={{0,128},{64,192},{128,0},{192,64},{1,129},{65,193},{129,1},{193,65... | collective-permute-start | bytes 49160 | tf_op jit(solution)/shard_map/ppermute | solution.py:283
  91.3 4.9 %collective-permute-start.5 = (f32[32,128]{1,0:T(8,128)S(1)}, f32[32,128]{1,0:T(8,128)S(1)}, u32[]{:S(2)}, u32[]{:S(2)}) collective-permute-start(f32[32,128]{1,0:T(8,128)S(1)} %shard_map.92), channel_id=1, source_target_pairs={{0,64},{64,128},{128,192},{192,0},{1,65},{65,129},{129,193},{193,1... | collective-permute-start | bytes 49160 | tf_op jit(solution)/shard_map/ppermute | solution.py:283
  96.4 21.0 %copy-start = (bf16[256,1024]{1,0:T(8,128)(2,1)S(1)}, bf16[256,1024]{1,0:T(8,128)(2,1)}, u32[]{:S(2)}) copy-start(bf16[256,1024]{1,0:T(8,128)(2,1)} %k_ref.1) | copy-start | bytes 1572868
  96.4 21.0 %copy-start.1 = (bf16[256,1024]{1,0:T(8,128)(2,1)S(1)}, bf16[256,1024]{1,0:T(8,128)(2,1)}, u32[]{:S(2)}) copy-start(bf16[256,1024]{1,0:T(8,128)(2,1)} %v_ref.1) | copy-start | bytes 1572868

commit v4 on v3

--- a/solution.py
+++ b/solution.py
@@ -18,7 +18,7 @@
 ROWS = HEADS * E // PEERS
 PER_HEAD = PEERS // HEADS
 SPAN = ROWS + 1
-PIECES = 4
+PIECES = 1
 SCALING = 1.0 / math.sqrt(E)
 F32 = jnp.float32
 BF16 = jnp.bfloat16
@@ -310,7 +310,7 @@
         k, v, log_decay, flops=2 * HEADS * T * E * E, hbm_in=(0, 1, 2), hbm_out=(0, 1, 2),
         scratch=[
             narrow, narrow, pltpu.VMEM((HEADS, T), F32), pltpu.VMEM((PEERS * SPAN, E), F32),
-            pltpu.VMEM((HEADS, T), F32), pltpu.VMEM((T, HEADS), F32), sems, sems, two, sems,
+            pltpu.VMEM((HEADS, T), F32), pltpu.VMEM((T, HEADS), F32), sems, sems, two, pltpu.SemaphoreType.DMA((3,)),
         ],
     )
     recv = exchanged(sent.reshape(PEERS, 1, SPAN * E)).reshape(PEERS * SPAN, E)

time: 120 us -> 120 us (level)
  no operation moved by 1% of the time
where the time goes in v4:
time: 120 us; the launch traced here: 119 us
  blocking collectives  42.4 us (35%)
  waiting for transfers between devices  33.5 us (28%)
  starting transfers between devices  25.4 us (21%)
  Pallas kernels  16.3 us (14%)
    all_to_all x2, blocking collectives, exchanged(): return lax.all_to_all(array, GROUP, 0, 0, tiled=True)  42.4 us
    all_to_all x2, waiting for transfers between devices, exchanged(): return lax.all_to_all(array, GROUP, 0, 0, tiled=True)  24.4 us
    all_to_all x2, starting transfers between devices, exchanged(): return lax.all_to_all(array, GROUP, 0, 0, tiled=True)  16.3 us
    pallas_call x11, Pallas kernels, call(): pl.pallas_call(kernel, out_shape=[pltpu.HBM(s, d) if i in hbm_out else ja...  16.3 us
    ppermute x6, starting transfers between devices, shifted(): return lax.ppermute(array, 'y', [(i, (i + by) % 4) for i in range(4)])  8.93 us
    ppermute x6, waiting for transfers between devices, shifted(): return lax.ppermute(array, 'y', [(i, (i + by) % 4) for i in range(4)])  6.7 us
  transfers between devices with their start and end apart: 10, of which 9 were waited for; matrix products, arithmetic and copies ran while one was open for 0% of the time, Pallas kernels for 7%

profile of v4, /device:TPU:32, one launch (start us, length us, event | category | flops | bytes accessed | tf_op | source)
XLA Modules:
  0.0 119.4 jit_solution(6367216114738807600)
XLA Ops:
  0.6 2.9 %shard_map.84 = (f32[1056,128]{1,0:T(8,128)}, f32[8,256]{1,0:T(8,128)}, f32[256,8]{1,0:T(8,128)}) custom-call(bf16[256,1024]{1,0:T(8,128)(2,1)} %k_ref.1, bf16[256,1024]{1,0:T(8,128)(2,1)} %v_ref.1, f32[8,256]{1,0:T(8,128)} %decay_hbm.1), custom_call_target="tpu_custom_call" | custom-call | flops 67108864 | bytes 1613824 | tf_op jit(solution)/shard_map/pallas_call | solution.py:51
  3.6 11.3 %all-to-all-start = ((f32[32,1,4224]{2,1,0:T(1,128)}), f32[32,1,4224]{2,1,0:T(1,128)S(1)}, u32[]{:S(2)}, u32[]{:S(2)}) async-start(f32[32,1,4224]{2,1,0:T(1,128)} %bitcast.12), calls=%async_computation | async-start | bytes 1081344 | tf_op jit(solution)/shard_map/all_to_all | solution.py:291
  14.9 3.2 %shard_map.85 = (bf16[8,256,256]{2,1,0:T(8,128)(2,1)}, f32[256,1024]{1,0:T(8,128)S(1)}, bf16[256,1024]{1,0:T(8,128)(2,1)S(1)}) custom-call(bf16[256,1024]{1,0:T(8,128)(2,1)} %q_hbm.3, bf16[256,1024]{1,0:T(8,128)(2,1)} %k_ref.1, bf16[256,1024]{1,0:T(8,128)(2,1)} %v_ref.1, f32[8,256]{1,0:T(8,128)S(1)} %copy-done.7, f32[256,8]{1,0:T(8,128)S(1)} %copy-done.2), custom_call_target="tpu_custom_call" | custom-call | flops 268435456 | bytes 4210688 | tf_op jit(solution)/shard_map/pallas_call | solution.py:51
  18.2 14.7 %all-to-all-done = f32[32,1,4224]{2,1,0:T(1,128)S(1)} async-done(((f32[32,1,4224]{2,1,0:T(1,128)}), f32[32,1,4224]{2,1,0:T(1,128)S(1)}, u32[]{:S(2)}, u32[]{:S(2)}) %all-to-all-start) | async-done | bytes 540704 | tf_op jit(solution)/shard_map/all_to_all | solution.py:291
  33.0 1.2 collective-permute-done.refs_1_.refs_3_.refs_5_.refs_9_
  34.2 1.7 %collective-permute-start.3 = (f32[40,128]{1,0:T(8,128)S(1)}, f32[40,128]{1,0:T(8,128)S(1)}, u32[]{:S(2)}, u32[]{:S(2)}) collective-permute-start(f32[40,128]{1,0:T(8,128)S(1)} %shard_map.87), channel_id=1, source_target_pairs={{0,64},{64,128},{128,192},{192,0},{1,65},{65,129},{129,193},{193,1... | collective-permute-start | bytes 61448 | tf_op jit(solution)/shard_map/ppermute | solution.py:283
  35.9 2.9 %collective-permute-start.2 = (f32[40,128]{1,0:T(8,128)S(1)}, f32[40,128]{1,0:T(8,128)S(1)}, u32[]{:S(2)}, u32[]{:S(2)}) collective-permute-start(f32[40,128]{1,0:T(8,128)S(1)} %shard_map.87), channel_id=1, source_target_pairs={{0,128},{64,192},{128,0},{192,64},{1,129},{65,193},{129,1},{193,65... | collective-permute-start | bytes 61448 | tf_op jit(solution)/shard_map/ppermute | solution.py:283
  38.8 1.3 %collective-permute-start.1 = (f32[40,128]{1,0:T(8,128)S(1)}, f32[40,128]{1,0:T(8,128)S(1)}, u32[]{:S(2)}, u32[]{:S(2)}) collective-permute-start(f32[40,128]{1,0:T(8,128)S(1)} %shard_map.87), channel_id=1, source_target_pairs={{0,192},{64,0},{128,64},{192,128},{1,193},{65,1},{129,65},{193,129... | collective-permute-start | bytes 61448 | tf_op jit(solution)/shard_map/ppermute | solution.py:283
  40.1 1.0 collective-permute-done.2.refs_3_.refs_7_
  41.1 1.4 %collective-permute-done.1.refs_2_.refs_6_.refs_8_ = f32[40,128]{1,0:T(8,128)S(1)} collective-permute-done((f32[40,128]{1,0:T(8,128)S(1)}, f32[40,128]{1,0:T(8,128)S(1)}, u32[]{:S(2)}, u32[]{:S(2)}) %collective-permute-start.1) | collective-permute-done | bytes 20512 | tf_op jit(solution)/shard_map/ppermute | solution.py:283
  42.6 21.4 %all_to_all.20 = f32[32,32,128]{2,1,0:T(8,128)S(1)} all-to-all(f32[32,32,128]{2,1,0:T(8,128)S(1)} %shard_map.88), channel_id=1, replica_groups=mesh['y'=4,'core'=2,'x'=4,'z'=8] {'x','z'}, dimensions={0} | all-to-all | bytes 1048576 | tf_op jit(solution)/shard_map/all_to_all | solution.py:291
  64.0 2.2 %shard_map.89 = (bf16[256,1024]{1,0:T(8,128)(2,1)}, bf16[256,1024]{1,0:T(8,128)(2,1)}, f32[8,128,128]{2,1,0:T(8,128)}, bf16[8,128,128]{2,1,0:T(8,128)(2,1)}) custom-call(f32[256,1024]{1,0:T(8,128)S(1)} %get-tuple-element.32.mixed_ref, bf16[256,1024]{1,0:T(8,128)(2,1)S(1)} %get-tuple-element.33.query_dec_ref, bf16[256,1024]{1,0:T(8,128)(2,1)S(1)} %copy-done.4, ...), custom_call_target="tpu_custom_call" | custom-call | flops 134217728 | bytes 4456448 | tf_op jit(solution)/shard_map/pallas_call | solution.py:51
  66.2 5.0 %all-to-all-start.2 = ((f32[32,32,128]{2,1,0:T(8,128)}), f32[32,32,128]{2,1,0:T(8,128)S(1)}, u32[]{:S(2)}, u32[]{:S(2)}) async-start(f32[32,32,128]{2,1,0:T(8,128)} %bitcast.13), calls=%async_computation.2 | async-start | bytes 1048576 | tf_op jit(solution)/shard_map/all_to_all | solution.py:291
  71.2 5.2 %shard_map.90 = (bf16[256,1024]{1,0:T(8,128)(2,1)}, f32[256,1024]{1,0:T(8,128)S(1)}, f32[256,1024]{1,0:T(8,128)S(1)}) custom-call(bf16[256,1024]{1,0:T(8,128)(2,1)} %q_hbm.3, bf16[256,1024]{1,0:T(8,128)(2,1)} %k_ref.1, bf16[256,1024]{1,0:T(8,128)(2,1)} %v_ref.1, bf16[8,256,256]{2,1,0:T(8,128)(2,1)} %get-tuple-element.38.weights_hbm, f32[8,256]{1,0:T(8,128)S(1)} %copy-done.7, ...), custom_call_target="tpu_custom_call" | custom-call | flops 603979776 | bytes 6045696 | tf_op jit(solution)/shard_map/pallas_call | solution.py:51
  76.5 1.0 copy-done.3
  77.5 9.7 %all-to-all-done.2 = f32[32,32,128]{2,1,0:T(8,128)S(1)} async-done(((f32[32,32,128]{2,1,0:T(8,128)}), f32[32,32,128]{2,1,0:T(8,128)S(1)}, u32[]{:S(2)}, u32[]{:S(2)}) %all-to-all-start.2) | async-done | bytes 524320 | tf_op jit(solution)/shard_map/all_to_all | solution.py:291
  87.4 1.2 collective-permute-done.4.refs_1_.refs_5_
  88.6 1.6 %collective-permute-start.7 = (f32[32,128]{1,0:T(8,128)S(1)}, f32[32,128]{1,0:T(8,128)S(1)}, u32[]{:S(2)}, u32[]{:S(2)}) collective-permute-start(f32[32,128]{1,0:T(8,128)S(1)} %shard_map.92), channel_id=1, source_target_pairs={{0,192},{64,0},{128,64},{192,128},{1,193},{65,1},{129,65},{193,129... | collective-permute-start | bytes 49160 | tf_op jit(solution)/shard_map/ppermute | solution.py:283
  90.2 0.7 collective-permute-start.6
  90.9 0.7 collective-permute-start.5
  91.6 0.8 collective-permute-done.7.refs_4_
  92.4 3.1 %collective-permute-done.6.refs_3_ = f32[32,128]{1,0:T(8,128)S(1)} collective-permute-done((f32[32,128]{1,0:T(8,128)S(1)}, f32[32,128]{1,0:T(8,128)S(1)}, u32[]{:S(2)}, u32[]{:S(2)}) %collective-permute-start.6) | collective-permute-done | bytes 16416 | tf_op jit(solution)/shard_map/ppermute | solution.py:283
  96.0 21.0 %all_to_all.21 = f32[32,32,128]{2,1,0:T(8,128)S(1)} all-to-all(f32[32,32,128]{2,1,0:T(8,128)S(1)} %shard_map.93), channel_id=1, replica_groups=mesh['y'=4,'core'=2,'x'=4,'z'=8] {'x','z'}, dimensions={0} | all-to-all | bytes 1048576 | tf_op jit(solution)/shard_map/all_to_all | solution.py:291
  117.0 2.4 %shard_map.94 = (bf16[256,1024]{1,0:T(8,128)(2,1)}, bf16[256,1024]{1,0:T(8,128)(2,1)}) custom-call(bf16[256,1024]{1,0:T(8,128)(2,1)S(1)} %copy-done, bf16[256,1024]{1,0:T(8,128)(2,1)S(1)} %copy-done.1, f32[256,8]{1,0:T(8,128)S(1)} %copy-done.2, f32[256,1024]{1,0:T(8,128)S(1)} %get-tuple-element.45.part_k_ref, f32[256,1024]{1,0:T(8,128)} %copy-done.3, ...), custom_call_target="tpu_custom_call" | custom-call | flops 134217728 | bytes 4726784 | tf_op jit(solution)/shard_map/pallas_call | solution.py:51
  (25 shorter events, 1.0 us)
Async XLA Ops:
  3.5 11.4 %copy-start.2 = (f32[256,8]{1,0:T(8,128)S(1)}, f32[256,8]{1,0:T(8,128)}, u32[]{:S(2)}) copy-start(f32[256,8]{1,0:T(8,128)} %get-tuple-element.29.run_col_ref) | copy-start | bytes 24580
  3.6 11.4 %copy-start.7 = (f32[8,256]{1,0:T(8,128)S(1)}, f32[8,256]{1,0:T(8,128)}, u32[]{:S(2)}) copy-start(f32[8,256]{1,0:T(8,128)} %get-tuple-element.28.run_row_ref) | copy-start | bytes 24580
  3.6 29.3 %all-to-all-start = ((f32[32,1,4224]{2,1,0:T(1,128)}), f32[32,1,4224]{2,1,0:T(1,128)S(1)}, u32[]{:S(2)}, u32[]{:S(2)}) async-start(f32[32,1,4224]{2,1,0:T(1,128)} %bitcast.12), calls=%async_computation | async-start | bytes 1081344 | tf_op jit(solution)/shard_map/all_to_all | solution.py:291
  32.9 1.3 %collective-permute-start = (f32[40,128]{1,0:T(8,128)S(1)}, f32[40,128]{1,0:T(8,128)S(1)}, u32[]{:S(2)}, u32[]{:S(2)}) collective-permute-start(f32[40,128]{1,0:T(8,128)S(1)} %get-tuple-element.36.refs_0_.refs_2_), channel_id=1, source_target_pairs={{0,32},{32,0},{1,33},{33,1},{2,34},{34,2},{3,35},{35,3},{4,36},{36... | collective-permute-start | bytes 61448 | tf_op jit(solution)/shard_map/ppermute | solution.py:287
  34.2 5.9 %collective-permute-start.3 = (f32[40,128]{1,0:T(8,128)S(1)}, f32[40,128]{1,0:T(8,128)S(1)}, u32[]{:S(2)}, u32[]{:S(2)}) collective-permute-start(f32[40,128]{1,0:T(8,128)S(1)} %shard_map.87), channel_id=1, source_target_pairs={{0,64},{64,128},{128,192},{192,0},{1,65},{65,129},{129,193},{193,1... | collective-permute-start | bytes 61448 | tf_op jit(solution)/shard_map/ppermute | solution.py:283
  35.9 5.3 %collective-permute-start.2 = (f32[40,128]{1,0:T(8,128)S(1)}, f32[40,128]{1,0:T(8,128)S(1)}, u32[]{:S(2)}, u32[]{:S(2)}) collective-permute-start(f32[40,128]{1,0:T(8,128)S(1)} %shard_map.87), channel_id=1, source_target_pairs={{0,128},{64,192},{128,0},{192,64},{1,129},{65,193},{129,1},{193,65... | collective-permute-start | bytes 61448 | tf_op jit(solution)/shard_map/ppermute | solution.py:283
  38.8 3.8 %collective-permute-start.1 = (f32[40,128]{1,0:T(8,128)S(1)}, f32[40,128]{1,0:T(8,128)S(1)}, u32[]{:S(2)}, u32[]{:S(2)}) collective-permute-start(f32[40,128]{1,0:T(8,128)S(1)} %shard_map.87), channel_id=1, source_target_pairs={{0,192},{64,0},{128,64},{192,128},{1,193},{65,1},{129,65},{193,129... | collective-permute-start | bytes 61448 | tf_op jit(solution)/shard_map/ppermute | solution.py:283
  42.6 21.4 %copy-start.4 = (bf16[256,1024]{1,0:T(8,128)(2,1)S(1)}, bf16[256,1024]{1,0:T(8,128)(2,1)}, u32[]{:S(2)}) copy-start(bf16[256,1024]{1,0:T(8,128)(2,1)} %g_ref.1) | copy-start | bytes 1572868
  66.2 5.0 %copy-start.5 = (bf16[256,1024]{1,0:T(8,128)(2,1)S(1)}, bf16[256,1024]{1,0:T(8,128)(2,1)}, u32[]{:S(2)}) copy-start(bf16[256,1024]{1,0:T(8,128)(2,1)} %get-tuple-element.39.grad_mixed_ref) | copy-start | bytes 1572868
  66.2 5.0 %copy-start.6 = (bf16[8,128,128]{2,1,0:T(8,128)(2,1)S(1)}, bf16[8,128,128]{2,1,0:T(8,128)(2,1)}, u32[]{:S(2)}) copy-start(bf16[8,128,128]{2,1,0:T(8,128)(2,1)} %get-tuple-element.40.half_ref) | copy-start | bytes 786436
  66.2 21.0 %all-to-all-start.2 = ((f32[32,32,128]{2,1,0:T(8,128)}), f32[32,32,128]{2,1,0:T(8,128)S(1)}, u32[]{:S(2)}, u32[]{:S(2)}) async-start(f32[32,32,128]{2,1,0:T(8,128)} %bitcast.13), calls=%async_computation.2 | async-start | bytes 1048576 | tf_op jit(solution)/shard_map/all_to_all | solution.py:291
  76.5 1.0 copy-start.3
  87.3 1.3 %collective-permute-start.4 = (f32[32,128]{1,0:T(8,128)S(1)}, f32[32,128]{1,0:T(8,128)S(1)}, u32[]{:S(2)}, u32[]{:S(2)}) collective-permute-start(f32[32,128]{1,0:T(8,128)S(1)} %shard_map.91.refs_0_), channel_id=1, source_target_pairs={{0,32},{32,0},{1,33},{33,1},{2,34},{34,2},{3,35},{35,3},{4,36},{36... | collective-permute-start | bytes 49160 | tf_op jit(solution)/shard_map/ppermute | solution.py:287
  88.6 3.8 %collective-permute-start.7 = (f32[32,128]{1,0:T(8,128)S(1)}, f32[32,128]{1,0:T(8,128)S(1)}, u32[]{:S(2)}, u32[]{:S(2)}) collective-permute-start(f32[32,128]{1,0:T(8,128)S(1)} %shard_map.92), channel_id=1, source_target_pairs={{0,192},{64,0},{128,64},{192,128},{1,193},{65,1},{129,65},{193,129... | collective-permute-start | bytes 49160 | tf_op jit(solution)/shard_map/ppermute | solution.py:283
  90.2 5.2 %collective-permute-start.6 = (f32[32,128]{1,0:T(8,128)S(1)}, f32[32,128]{1,0:T(8,128)S(1)}, u32[]{:S(2)}, u32[]{:S(2)}) collective-permute-start(f32[32,128]{1,0:T(8,128)S(1)} %shard_map.92), channel_id=1, source_target_pairs={{0,128},{64,192},{128,0},{192,64},{1,129},{65,193},{129,1},{193,65... | collective-permute-start | bytes 49160 | tf_op jit(solution)/shard_map/ppermute | solution.py:283
  90.9 4.9 %collective-permute-start.5 = (f32[32,128]{1,0:T(8,128)S(1)}, f32[32,128]{1,0:T(8,128)S(1)}, u32[]{:S(2)}, u32[]{:S(2)}) collective-permute-start(f32[32,128]{1,0:T(8,128)S(1)} %shard_map.92), channel_id=1, source_target_pairs={{0,64},{64,128},{128,192},{192,0},{1,65},{65,129},{129,193},{193,1... | collective-permute-start | bytes 49160 | tf_op jit(solution)/shard_map/ppermute | solution.py:283
  96.0 21.0 %copy-start = (bf16[256,1024]{1,0:T(8,128)(2,1)S(1)}, bf16[256,1024]{1,0:T(8,128)(2,1)}, u32[]{:S(2)}) copy-start(bf16[256,1024]{1,0:T(8,128)(2,1)} %k_ref.1) | copy-start | bytes 1572868
  96.0 21.0 %copy-start.1 = (bf16[256,1024]{1,0:T(8,128)(2,1)S(1)}, bf16[256,1024]{1,0:T(8,128)(2,1)}, u32[]{:S(2)}) copy-start(bf16[256,1024]{1,0:T(8,128)(2,1)} %v_ref.1) | copy-start | bytes 1572868

commit v5 on v4

--- a/solution.py
+++ b/solution.py
@@ -151,13 +151,11 @@
 
 
 def mixed_kernel(
-    mixed_ref, query_dec_ref, g_ref, entering_ref, attended_hbm, grad_mixed_hbm, state_hbm, half_hbm,
-    attended_ref, grad_mixed_ref, state_ref, half_ref, attended_sem, grad_mixed_sem, state_sem, half_sem,
+    mixed_ref, query_dec_ref, g_ref, entering_ref, attended_ref, grad_mixed_ref, state_hbm, half_hbm,
+    state_ref, half_ref, state_sem, half_sem,
 ):
     def send(half):
-        tall = [(state_ref, state_hbm, state_sem), (half_ref, half_hbm, half_sem)]
-        wide = [(attended_ref, attended_hbm, attended_sem), (grad_mixed_ref, grad_mixed_hbm, grad_mixed_sem)]
-        return half_copies(tall, half, False) + half_copies(wide, half, True)
+        return half_copies([(state_ref, state_hbm, state_sem), (half_ref, half_hbm, half_sem)], half, False)
 
     for half in range(2):
         for h in range(half * HEADS // 2, (half + 1) * HEADS // 2):
@@ -179,10 +177,12 @@
 
 
 def local_grads_kernel(
-    q_hbm, k_hbm, v_hbm, weights_hbm, run_row_ref, run_col_ref, grad_mixed_ref, half_ref,
-    grad_q_hbm, part_k_ref, part_v_ref,
-    q_ref, k_ref, v_ref, weights_ref, grad_q_ref, q_sem, k_sem, v_sem, w_sem, out_sem,
-):
+    q_hbm, k_hbm, v_hbm, weights_hbm, run_row_ref, run_col_ref, grad_mixed_ref, half_ref, attended_ref,
+    grad_q_hbm, part_k_ref, part_v_ref, attended_hbm,
+    q_ref, k_ref, v_ref, weights_ref, grad_q_ref, q_sem, k_sem, v_sem, w_sem, out_sem, attended_sem,
+):
+    store_attended = pieces(attended_ref, attended_hbm, attended_sem)
+    start(store_attended)
     loads = pieces(q_hbm, q_ref, q_sem) + pieces(k_hbm, k_ref, k_sem)
     loads += pieces(v_hbm, v_ref, v_sem) + pieces(weights_hbm, weights_ref, w_sem)
     start(loads)
@@ -202,30 +202,32 @@
         part_v_ref[:, lanes(h)] = dot(weights_ref[h], grad_mixed, TN)
     stores = pieces(grad_q_ref, grad_q_hbm, out_sem)
     start(stores)
-    wait(stores)
+    wait(stores + store_attended)
 
 
 def final_kernel(
     k_ref, v_ref, run_col_ref, part_k_ref, part_v_hbm, leaving_ref, grad_k_hbm, grad_v_hbm,
     part_v_ref, grad_k_ref, grad_v_ref, in_sem, k_sem, v_sem,
 ):
-    loads = pieces(part_v_hbm, part_v_ref, in_sem)
-    start(loads)
+    loads = [half_copies([(part_v_hbm, part_v_ref, in_sem)], half, True) for half in range(2)]
+    start(loads[0] + loads[1])
     run_col = run_col_ref[...]
     shrink = jnp.exp(run_col[T - 1 : T, :] - run_col)
     for h in range(HEADS):
         grad_k = shrink[:, h : h + 1] * dot(v_ref[:, lanes(h)], leaving_ref[h].astype(BF16), NT)
         grad_k_ref[:, lanes(h)] = (part_k_ref[:, lanes(h)] + grad_k).astype(BF16)
-    store_k = pieces(grad_k_ref, grad_k_hbm, k_sem)
-    start(store_k)
-    wait(loads)
-    for h in range(HEADS):
-        key_dec = (k_ref[:, lanes(h)].astype(F32) * shrink[:, h : h + 1]).astype(BF16)
-        grad_v = dot(key_dec, leaving_ref[h].astype(BF16), NN)
-        grad_v_ref[:, lanes(h)] = (part_v_ref[:, lanes(h)] + grad_v).astype(BF16)
-    store_v = pieces(grad_v_ref, grad_v_hbm, v_sem)
-    start(store_v)
-    wait(store_k + store_v)
+    stores = pieces(grad_k_ref, grad_k_hbm, k_sem)
+    start(stores)
+    for half in range(2):
+        wait(loads[half])
+        for h in range(half * HEADS // 2, (half + 1) * HEADS // 2):
+            key_dec = (k_ref[:, lanes(h)].astype(F32) * shrink[:, h : h + 1]).astype(BF16)
+            grad_v = dot(key_dec, leaving_ref[h].astype(BF16), NN)
+            grad_v_ref[:, lanes(h)] = (part_v_ref[:, lanes(h)] + grad_v).astype(BF16)
+        store = half_copies([(grad_v_ref, grad_v_hbm, v_sem)], half, True)
+        start(store)
+        stores += store
+    wait(stores)
 
 
 def group_total_kernel(recv_ref, total_ref, decays_ref):
@@ -331,15 +333,15 @@
 
     attended, grad_mixed, state, half = call(
         mixed_kernel, [(wide, BF16), (wide, BF16), ((HEADS, E, E), F32), ((HEADS, E, E), BF16)],
-        mixed_part, query_dec, g, entering, flops=4 * HEADS * T * E * E, hbm_out=(0, 1, 2, 3),
-        scratch=[narrow, narrow, pltpu.VMEM((HEADS, E, E), F32), pltpu.VMEM((HEADS, E, E), BF16), two, two, two, two],
+        mixed_part, query_dec, g, entering, flops=4 * HEADS * T * E * E, hbm_out=(2, 3),
+        scratch=[pltpu.VMEM((HEADS, E, E), F32), pltpu.VMEM((HEADS, E, E), BF16), two, two],
     )
     recv = exchanged(state.reshape(PEERS, ROWS, E)).reshape(PEERS * ROWS, E)
-    grad_q, part_k, part_v = call(
-        local_grads_kernel, [(wide, BF16), (wide, F32), (wide, F32)],
-        q, k, v, weights, run_row, run_col, grad_mixed, half, flops=9 * HEADS * T * T * E,
-        hbm_in=(0, 1, 2, 3), hbm_out=(0,),
-        scratch=[narrow, narrow, narrow, square, narrow, sems, sems, sems, sems, sems],
+    grad_q, part_k, part_v, attended = call(
+        local_grads_kernel, [(wide, BF16), (wide, F32), (wide, F32), (wide, BF16)],
+        q, k, v, weights, run_row, run_col, grad_mixed, half, attended, flops=9 * HEADS * T * T * E,
+        hbm_in=(0, 1, 2, 3), hbm_out=(0, 3),
+        scratch=[narrow, narrow, narrow, square, narrow, sems, sems, sems, sems, sems, sems],
     )
     recv, part_k, part_v = lax.optimization_barrier((recv, part_k, part_v))
     back_total = call(back_total_kernel, [((ROWS, E), F32)], recv, decays)[0]
@@ -351,7 +353,7 @@
     grad_k, grad_v = call(
         final_kernel, [(wide, BF16), (wide, BF16)],
         k, v, run_col, part_k, part_v, leaving, flops=4 * HEADS * T * E * E, hbm_in=(4,), hbm_out=(0, 1),
-        scratch=[pltpu.VMEM(wide, F32), narrow, narrow, sems, sems, sems],
+        scratch=[pltpu.VMEM(wide, F32), narrow, narrow, two, sems, two],
     )
     return attended, grad_q, grad_k, grad_v
 

time: 120 us -> 120 us (level)
  no operation moved by 1% of the time
where the time goes in v5:
time: 120 us; the launch traced here: 119 us
  blocking collectives  42.4 us (35%)
  waiting for transfers between devices  33.3 us (28%)
  starting transfers between devices  25.4 us (21%)
  Pallas kernels  16.3 us (14%)
    all_to_all x2, blocking collectives, exchanged(): return lax.all_to_all(array, GROUP, 0, 0, tiled=True)  42.4 us
    all_to_all x2, waiting for transfers between devices, exchanged(): return lax.all_to_all(array, GROUP, 0, 0, tiled=True)  24.2 us
    all_to_all x2, starting transfers between devices, exchanged(): return lax.all_to_all(array, GROUP, 0, 0, tiled=True)  16.3 us
    pallas_call x11, Pallas kernels, call(): pl.pallas_call(kernel, out_shape=[pltpu.HBM(s, d) if i in hbm_out else ja...  16.3 us
    ppermute x6, starting transfers between devices, shifted(): return lax.ppermute(array, 'y', [(i, (i + by) % 4) for i in range(4)])  8.93 us
    ppermute x6, waiting for transfers between devices, shifted(): return lax.ppermute(array, 'y', [(i, (i + by) % 4) for i in range(4)])  6.7 us
  transfers between devices with their start and end apart: 10, of which 9 were waited for; matrix products, arithmetic and copies ran while one was open for 0% of the time, Pallas kernels for 7%

profile of v5, /device:TPU:32, one launch (start us, length us, event | category | flops | bytes accessed | tf_op | source)
XLA Modules:
  0.0 119.2 jit_solution(2149825490490968377)
XLA Ops:
  0.6 2.9 %shard_map.84 = (f32[1056,128]{1,0:T(8,128)}, f32[8,256]{1,0:T(8,128)}, f32[256,8]{1,0:T(8,128)}) custom-call(bf16[256,1024]{1,0:T(8,128)(2,1)} %k_ref.1, bf16[256,1024]{1,0:T(8,128)(2,1)} %v_ref.1, f32[8,256]{1,0:T(8,128)} %decay_hbm.1), custom_call_target="tpu_custom_call" | custom-call | flops 67108864 | bytes 1613824 | tf_op jit(solution)/shard_map/pallas_call | solution.py:51
  3.6 11.3 %all-to-all-start = ((f32[32,1,4224]{2,1,0:T(1,128)}), f32[32,1,4224]{2,1,0:T(1,128)S(1)}, u32[]{:S(2)}, u32[]{:S(2)}) async-start(f32[32,1,4224]{2,1,0:T(1,128)} %bitcast.12), calls=%async_computation | async-start | bytes 1081344 | tf_op jit(solution)/shard_map/all_to_all | solution.py:293
  14.9 3.2 %shard_map.85 = (bf16[8,256,256]{2,1,0:T(8,128)(2,1)}, f32[256,1024]{1,0:T(8,128)S(1)}, bf16[256,1024]{1,0:T(8,128)(2,1)S(1)}) custom-call(bf16[256,1024]{1,0:T(8,128)(2,1)} %q_hbm.3, bf16[256,1024]{1,0:T(8,128)(2,1)} %k_ref.1, bf16[256,1024]{1,0:T(8,128)(2,1)} %v_ref.1, f32[8,256]{1,0:T(8,128)S(1)} %copy-done.6, f32[256,8]{1,0:T(8,128)S(1)} %copy-done.2), custom_call_target="tpu_custom_call" | custom-call | flops 268435456 | bytes 4210688 | tf_op jit(solution)/shard_map/pallas_call | solution.py:51
  18.2 14.7 %all-to-all-done = f32[32,1,4224]{2,1,0:T(1,128)S(1)} async-done(((f32[32,1,4224]{2,1,0:T(1,128)}), f32[32,1,4224]{2,1,0:T(1,128)S(1)}, u32[]{:S(2)}, u32[]{:S(2)}) %all-to-all-start) | async-done | bytes 540704 | tf_op jit(solution)/shard_map/all_to_all | solution.py:293
  33.0 1.2 collective-permute-done.refs_1_.refs_3_.refs_5_.refs_9_
  34.2 1.7 %collective-permute-start.3 = (f32[40,128]{1,0:T(8,128)S(1)}, f32[40,128]{1,0:T(8,128)S(1)}, u32[]{:S(2)}, u32[]{:S(2)}) collective-permute-start(f32[40,128]{1,0:T(8,128)S(1)} %shard_map.87), channel_id=1, source_target_pairs={{0,64},{64,128},{128,192},{192,0},{1,65},{65,129},{129,193},{193,1... | collective-permute-start | bytes 61448 | tf_op jit(solution)/shard_map/ppermute | solution.py:285
  35.8 2.9 %collective-permute-start.2 = (f32[40,128]{1,0:T(8,128)S(1)}, f32[40,128]{1,0:T(8,128)S(1)}, u32[]{:S(2)}, u32[]{:S(2)}) collective-permute-start(f32[40,128]{1,0:T(8,128)S(1)} %shard_map.87), channel_id=1, source_target_pairs={{0,128},{64,192},{128,0},{192,64},{1,129},{65,193},{129,1},{193,65... | collective-permute-start | bytes 61448 | tf_op jit(solution)/shard_map/ppermute | solution.py:285
  38.7 1.3 %collective-permute-start.1 = (f32[40,128]{1,0:T(8,128)S(1)}, f32[40,128]{1,0:T(8,128)S(1)}, u32[]{:S(2)}, u32[]{:S(2)}) collective-permute-start(f32[40,128]{1,0:T(8,128)S(1)} %shard_map.87), channel_id=1, source_target_pairs={{0,192},{64,0},{128,64},{192,128},{1,193},{65,1},{129,65},{193,129... | collective-permute-start | bytes 61448 | tf_op jit(solution)/shard_map/ppermute | solution.py:285
  40.1 1.0 collective-permute-done.2.refs_3_.refs_7_
  41.1 1.4 %collective-permute-done.1.refs_2_.refs_6_.refs_8_ = f32[40,128]{1,0:T(8,128)S(1)} collective-permute-done((f32[40,128]{1,0:T(8,128)S(1)}, f32[40,128]{1,0:T(8,128)S(1)}, u32[]{:S(2)}, u32[]{:S(2)}) %collective-permute-start.1) | collective-permute-done | bytes 20512 | tf_op jit(solution)/shard_map/ppermute | solution.py:285
  42.6 21.3 %all_to_all.20 = f32[32,32,128]{2,1,0:T(8,128)S(1)} all-to-all(f32[32,32,128]{2,1,0:T(8,128)S(1)} %shard_map.88), channel_id=1, replica_groups=mesh['y'=4,'core'=2,'x'=4,'z'=8] {'x','z'}, dimensions={0} | all-to-all | bytes 1048576 | tf_op jit(solution)/shard_map/all_to_all | solution.py:293
  64.0 2.1 %shard_map.89 = (bf16[256,1024]{1,0:T(8,128)(2,1)S(1)}, bf16[256,1024]{1,0:T(8,128)(2,1)S(1)}, f32[8,128,128]{2,1,0:T(8,128)}, bf16[8,128,128]{2,1,0:T(8,128)(2,1)}) custom-call(f32[256,1024]{1,0:T(8,128)S(1)} %get-tuple-element.34.mixed_ref, bf16[256,1024]{1,0:T(8,128)(2,1)S(1)} %get-tuple-element.35.query_dec_ref, bf16[256,1024]{1,0:T(8,128)(2,1)S(1)} %copy-done.4, ...), custom_call_target="tpu_custom_call" | custom-call | flops 134217728 | bytes 4456448 | tf_op jit(solution)/shard_map/pallas_call | solution.py:51
  66.1 5.0 %all-to-all-start.2 = ((f32[32,32,128]{2,1,0:T(8,128)}), f32[32,32,128]{2,1,0:T(8,128)S(1)}, u32[]{:S(2)}, u32[]{:S(2)}) async-start(f32[32,32,128]{2,1,0:T(8,128)} %bitcast.13), calls=%async_computation.2 | async-start | bytes 1048576 | tf_op jit(solution)/shard_map/all_to_all | solution.py:293
  71.1 5.4 %shard_map.90 = (bf16[256,1024]{1,0:T(8,128)(2,1)}, f32[256,1024]{1,0:T(8,128)S(1)}, f32[256,1024]{1,0:T(8,128)S(1)}, bf16[256,1024]{1,0:T(8,128)(2,1)}) custom-call(bf16[256,1024]{1,0:T(8,128)(2,1)} %q_hbm.3, bf16[256,1024]{1,0:T(8,128)(2,1)} %k_ref.1, bf16[256,1024]{1,0:T(8,128)(2,1)} %v_ref.1, bf16[8,256,256]{2,1,0:T(8,128)(2,1)} %get-tuple-element.30.weights_hbm, ...), custom_call_target="tpu_custom_call" | custom-call | flops 603979776 | bytes 7094272 | tf_op jit(solution)/shard_map/pallas_call | solution.py:51
  76.6 1.0 copy-done.3
  77.5 9.6 %all-to-all-done.2 = f32[32,32,128]{2,1,0:T(8,128)S(1)} async-done(((f32[32,32,128]{2,1,0:T(8,128)}), f32[32,32,128]{2,1,0:T(8,128)S(1)}, u32[]{:S(2)}, u32[]{:S(2)}) %all-to-all-start.2) | async-done | bytes 524320 | tf_op jit(solution)/shard_map/all_to_all | solution.py:293
  87.3 1.2 collective-permute-done.4.refs_1_.refs_5_
  88.5 1.6 %collective-permute-start.7 = (f32[32,128]{1,0:T(8,128)S(1)}, f32[32,128]{1,0:T(8,128)S(1)}, u32[]{:S(2)}, u32[]{:S(2)}) collective-permute-start(f32[32,128]{1,0:T(8,128)S(1)} %shard_map.92), channel_id=1, source_target_pairs={{0,192},{64,0},{128,64},{192,128},{1,193},{65,1},{129,65},{193,129... | collective-permute-start | bytes 49160 | tf_op jit(solution)/shard_map/ppermute | solution.py:285
  90.1 0.7 collective-permute-start.6
  90.8 0.7 collective-permute-start.5
  91.5 0.8 collective-permute-done.7.refs_4_
  92.3 3.1 %collective-permute-done.6.refs_3_ = f32[32,128]{1,0:T(8,128)S(1)} collective-permute-done((f32[32,128]{1,0:T(8,128)S(1)}, f32[32,128]{1,0:T(8,128)S(1)}, u32[]{:S(2)}, u32[]{:S(2)}) %collective-permute-start.6) | collective-permute-done | bytes 16416 | tf_op jit(solution)/shard_map/ppermute | solution.py:285
  95.9 21.0 %all_to_all.21 = f32[32,32,128]{2,1,0:T(8,128)S(1)} all-to-all(f32[32,32,128]{2,1,0:T(8,128)S(1)} %shard_map.93), channel_id=1, replica_groups=mesh['y'=4,'core'=2,'x'=4,'z'=8] {'x','z'}, dimensions={0} | all-to-all | bytes 1048576 | tf_op jit(solution)/shard_map/all_to_all | solution.py:293
  116.9 2.3 %shard_map.94 = (bf16[256,1024]{1,0:T(8,128)(2,1)}, bf16[256,1024]{1,0:T(8,128)(2,1)}) custom-call(bf16[256,1024]{1,0:T(8,128)(2,1)S(1)} %copy-done, bf16[256,1024]{1,0:T(8,128)(2,1)S(1)} %copy-done.1, f32[256,8]{1,0:T(8,128)S(1)} %copy-done.2, f32[256,1024]{1,0:T(8,128)S(1)} %get-tuple-element.47.part_k_ref, f32[256,1024]{1,0:T(8,128)} %copy-done.3, ...), custom_call_target="tpu_custom_call" | custom-call | flops 134217728 | bytes 4726784 | tf_op jit(solution)/shard_map/pallas_call | solution.py:51
  (23 shorter events, 1.0 us)
Async XLA Ops:
  3.5 11.4 %copy-start.2 = (f32[256,8]{1,0:T(8,128)S(1)}, f32[256,8]{1,0:T(8,128)}, u32[]{:S(2)}) copy-start(f32[256,8]{1,0:T(8,128)} %get-tuple-element.29.run_col_ref) | copy-start | bytes 24580
  3.6 11.4 %copy-start.6 = (f32[8,256]{1,0:T(8,128)S(1)}, f32[8,256]{1,0:T(8,128)}, u32[]{:S(2)}) copy-start(f32[8,256]{1,0:T(8,128)} %get-tuple-element.28.run_row_ref) | copy-start | bytes 24580
  3.6 29.3 %all-to-all-start = ((f32[32,1,4224]{2,1,0:T(1,128)}), f32[32,1,4224]{2,1,0:T(1,128)S(1)}, u32[]{:S(2)}, u32[]{:S(2)}) async-start(f32[32,1,4224]{2,1,0:T(1,128)} %bitcast.12), calls=%async_computation | async-start | bytes 1081344 | tf_op jit(solution)/shard_map/all_to_all | solution.py:293
  32.9 1.3 %collective-permute-start = (f32[40,128]{1,0:T(8,128)S(1)}, f32[40,128]{1,0:T(8,128)S(1)}, u32[]{:S(2)}, u32[]{:S(2)}) collective-permute-start(f32[40,128]{1,0:T(8,128)S(1)} %get-tuple-element.38.refs_0_.refs_2_), channel_id=1, source_target_pairs={{0,32},{32,0},{1,33},{33,1},{2,34},{34,2},{3,35},{35,3},{4,36},{36... | collective-permute-start | bytes 61448 | tf_op jit(solution)/shard_map/ppermute | solution.py:289
  34.2 5.9 %collective-permute-start.3 = (f32[40,128]{1,0:T(8,128)S(1)}, f32[40,128]{1,0:T(8,128)S(1)}, u32[]{:S(2)}, u32[]{:S(2)}) collective-permute-start(f32[40,128]{1,0:T(8,128)S(1)} %shard_map.87), channel_id=1, source_target_pairs={{0,64},{64,128},{128,192},{192,0},{1,65},{65,129},{129,193},{193,1... | collective-permute-start | bytes 61448 | tf_op jit(solution)/shard_map/ppermute | solution.py:285
  35.8 5.3 %collective-permute-start.2 = (f32[40,128]{1,0:T(8,128)S(1)}, f32[40,128]{1,0:T(8,128)S(1)}, u32[]{:S(2)}, u32[]{:S(2)}) collective-permute-start(f32[40,128]{1,0:T(8,128)S(1)} %shard_map.87), channel_id=1, source_target_pairs={{0,128},{64,192},{128,0},{192,64},{1,129},{65,193},{129,1},{193,65... | collective-permute-start | bytes 61448 | tf_op jit(solution)/shard_map/ppermute | solution.py:285
  38.7 3.8 %collective-permute-start.1 = (f32[40,128]{1,0:T(8,128)S(1)}, f32[40,128]{1,0:T(8,128)S(1)}, u32[]{:S(2)}, u32[]{:S(2)}) collective-permute-start(f32[40,128]{1,0:T(8,128)S(1)} %shard_map.87), channel_id=1, source_target_pairs={{0,192},{64,0},{128,64},{192,128},{1,193},{65,1},{129,65},{193,129... | collective-permute-start | bytes 61448 | tf_op jit(solution)/shard_map/ppermute | solution.py:285
  42.6 21.4 %copy-start.4 = (bf16[256,1024]{1,0:T(8,128)(2,1)S(1)}, bf16[256,1024]{1,0:T(8,128)(2,1)}, u32[]{:S(2)}) copy-start(bf16[256,1024]{1,0:T(8,128)(2,1)} %g_ref.1) | copy-start | bytes 1572868
  66.1 5.0 %copy-start.5 = (bf16[8,128,128]{2,1,0:T(8,128)(2,1)S(1)}, bf16[8,128,128]{2,1,0:T(8,128)(2,1)}, u32[]{:S(2)}) copy-start(bf16[8,128,128]{2,1,0:T(8,128)(2,1)} %get-tuple-element.40.half_ref) | copy-start | bytes 786436
  66.1 21.0 %all-to-all-start.2 = ((f32[32,32,128]{2,1,0:T(8,128)}), f32[32,32,128]{2,1,0:T(8,128)S(1)}, u32[]{:S(2)}, u32[]{:S(2)}) async-start(f32[32,32,128]{2,1,0:T(8,128)} %bitcast.13), calls=%async_computation.2 | async-start | bytes 1048576 | tf_op jit(solution)/shard_map/all_to_all | solution.py:293
  76.6 1.0 copy-start.3
  87.2 1.3 %collective-permute-start.4 = (f32[32,128]{1,0:T(8,128)S(1)}, f32[32,128]{1,0:T(8,128)S(1)}, u32[]{:S(2)}, u32[]{:S(2)}) collective-permute-start(f32[32,128]{1,0:T(8,128)S(1)} %shard_map.91.refs_0_), channel_id=1, source_target_pairs={{0,32},{32,0},{1,33},{33,1},{2,34},{34,2},{3,35},{35,3},{4,36},{36... | collective-permute-start | bytes 49160 | tf_op jit(solution)/shard_map/ppermute | solution.py:289
  88.5 3.8 %collective-permute-start.7 = (f32[32,128]{1,0:T(8,128)S(1)}, f32[32,128]{1,0:T(8,128)S(1)}, u32[]{:S(2)}, u32[]{:S(2)}) collective-permute-start(f32[32,128]{1,0:T(8,128)S(1)} %shard_map.92), channel_id=1, source_target_pairs={{0,192},{64,0},{128,64},{192,128},{1,193},{65,1},{129,65},{193,129... | collective-permute-start | bytes 49160 | tf_op jit(solution)/shard_map/ppermute | solution.py:285
  90.1 5.2 %collective-permute-start.6 = (f32[32,128]{1,0:T(8,128)S(1)}, f32[32,128]{1,0:T(8,128)S(1)}, u32[]{:S(2)}, u32[]{:S(2)}) collective-permute-start(f32[32,128]{1,0:T(8,128)S(1)} %shard_map.92), channel_id=1, source_target_pairs={{0,128},{64,192},{128,0},{192,64},{1,129},{65,193},{129,1},{193,65... | collective-permute-start | bytes 49160 | tf_op jit(solution)/shard_map/ppermute | solution.py:285
  90.8 4.9 %collective-permute-start.5 = (f32[32,128]{1,0:T(8,128)S(1)}, f32[32,128]{1,0:T(8,128)S(1)}, u32[]{:S(2)}, u32[]{:S(2)}) collective-permute-start(f32[32,128]{1,0:T(8,128)S(1)} %shard_map.92), channel_id=1, source_target_pairs={{0,64},{64,128},{128,192},{192,0},{1,65},{65,129},{129,193},{193,1... | collective-permute-start | bytes 49160 | tf_op jit(solution)/shard_map/ppermute | solution.py:285
  95.9 21.0 %copy-start = (bf16[256,1024]{1,0:T(8,128)(2,1)S(1)}, bf16[256,1024]{1,0:T(8,128)(2,1)}, u32[]{:S(2)}) copy-start(bf16[256,1024]{1,0:T(8,128)(2,1)} %k_ref.1) | copy-start | bytes 1572868
  95.9 21.0 %copy-start.1 = (bf16[256,1024]{1,0:T(8,128)(2,1)S(1)}, bf16[256,1024]{1,0:T(8,128)(2,1)}, u32[]{:S(2)}) copy-start(bf16[256,1024]{1,0:T(8,128)(2,1)} %v_ref.1) | copy-start | bytes 1572868

commit v6 on v5

--- a/solution.py
+++ b/solution.py
@@ -91,8 +91,8 @@
 
 
 def states_kernel(
-    k_hbm, v_hbm, decay_hbm, sent_hbm, run_row_hbm, run_col_hbm,
-    k_ref, v_ref, decay_ref, sent_ref, run_row_ref, run_col_ref, k_sem, v_sem, out_sem, small_sem,
+    k_hbm, v_hbm, decay_hbm, sent_hbm, run_row_ref, run_col_ref,
+    k_ref, v_ref, decay_ref, sent_ref, k_sem, v_sem, out_sem, small_sem,
 ):
     load_decay = pltpu.make_async_copy(decay_hbm, decay_ref, small_sem.at[0])
     loads = pieces(k_hbm, k_ref, k_sem) + pieces(v_hbm, v_ref, v_sem)
@@ -106,11 +106,6 @@
     run_row_ref[...] = run_row
     run_col_ref[...] = run_col
     totals = jnp.broadcast_to(run_row[:, T - 1 : T], (HEADS, E))
-    small = [
-        pltpu.make_async_copy(run_row_ref, run_row_hbm, small_sem.at[1]),
-        pltpu.make_async_copy(run_col_ref, run_col_hbm, small_sem.at[2]),
-    ]
-    start(small)
     shrink = jnp.exp(run_col[T - 1 : T, :] - run_col)
     wait(loads)
     for half in range(2):
@@ -122,7 +117,6 @@
                 sent_ref[row : row + ROWS] = state[i * ROWS : (i + 1) * ROWS]
                 sent_ref[row + ROWS : row + SPAN] = totals[h : h + 1]
         start(half_copies([(sent_ref, sent_hbm, out_sem)], half, False))
-    wait(small)
     for half in range(2):
         wait(half_copies([(sent_ref, sent_hbm, out_sem)], half, False))
 
@@ -309,10 +303,10 @@
 
     sent, run_row, run_col = call(
         states_kernel, [((PEERS * SPAN, E), F32), ((HEADS, T), F32), ((T, HEADS), F32)],
-        k, v, log_decay, flops=2 * HEADS * T * E * E, hbm_in=(0, 1, 2), hbm_out=(0, 1, 2),
+        k, v, log_decay, flops=2 * HEADS * T * E * E, hbm_in=(0, 1, 2), hbm_out=(0,),
         scratch=[
             narrow, narrow, pltpu.VMEM((HEADS, T), F32), pltpu.VMEM((PEERS * SPAN, E), F32),
-            pltpu.VMEM((HEADS, T), F32), pltpu.VMEM((T, HEADS), F32), sems, sems, two, pltpu.SemaphoreType.DMA((3,)),
+            sems, sems, two, pltpu.SemaphoreType.DMA((1,)),
         ],
     )
     recv = exchanged(sent.reshape(PEERS, 1, SPAN * E)).reshape(PEERS * SPAN, E)

time: 120 us -> 119 us (level)
  no operation moved by 1% of the time
where the time goes in v6:
time: 119 us
  blocking collectives  42.3 us (36%)
  waiting for transfers between devices  33.3 us (28%)
  starting transfers between devices  25.3 us (21%)
  Pallas kernels  16.3 us (14%)
    all_to_all x2, blocking collectives, exchanged(): return lax.all_to_all(array, GROUP, 0, 0, tiled=True)  42.3 us
    all_to_all x2, waiting for transfers between devices, exchanged(): return lax.all_to_all(array, GROUP, 0, 0, tiled=True)  24.2 us
    pallas_call x11, Pallas kernels, call(): pl.pallas_call(kernel, out_shape=[pltpu.HBM(s, d) if i in hbm_out else ja...  16.3 us
    all_to_all x2, starting transfers between devices, exchanged(): return lax.all_to_all(array, GROUP, 0, 0, tiled=True)  16.2 us
    ppermute x6, starting transfers between devices, shifted(): return lax.ppermute(array, 'y', [(i, (i + by) % 4) for i in range(4)])  8.94 us
    ppermute x6, waiting for transfers between devices, shifted(): return lax.ppermute(array, 'y', [(i, (i + by) % 4) for i in range(4)])  6.7 us
  transfers between devices with their start and end apart: 10, of which 9 were waited for; matrix products, arithmetic and copies ran while one was open for 0% of the time, Pallas kernels for 7%

profile of v6, /device:TPU:32, one launch (start us, length us, event | category | flops | bytes accessed | tf_op | source)
XLA Modules:
  0.0 119.0 jit_solution(17943904199641743014)
XLA Ops:
  0.6 2.9 %shard_map.84 = (f32[1056,128]{1,0:T(8,128)}, f32[8,256]{1,0:T(8,128)S(1)}, f32[256,8]{1,0:T(8,128)S(1)}) custom-call(bf16[256,1024]{1,0:T(8,128)(2,1)} %k_ref.1, bf16[256,1024]{1,0:T(8,128)(2,1)} %v_ref.1, f32[8,256]{1,0:T(8,128)} %decay_hbm.1), custom_call_target="tpu_custom_call" | custom-call | flops 67108864 | bytes 1613824 | tf_op jit(solution)/shard_map/pallas_call | solution.py:51
  3.5 11.2 %all-to-all-start = ((f32[32,1,4224]{2,1,0:T(1,128)}), f32[32,1,4224]{2,1,0:T(1,128)S(1)}, u32[]{:S(2)}, u32[]{:S(2)}) async-start(f32[32,1,4224]{2,1,0:T(1,128)} %bitcast.12), calls=%async_computation | async-start | bytes 1081344 | tf_op jit(solution)/shard_map/all_to_all | solution.py:287
  14.7 3.2 %shard_map.85 = (bf16[8,256,256]{2,1,0:T(8,128)(2,1)}, f32[256,1024]{1,0:T(8,128)S(1)}, bf16[256,1024]{1,0:T(8,128)(2,1)S(1)}) custom-call(bf16[256,1024]{1,0:T(8,128)(2,1)} %q_hbm.3, bf16[256,1024]{1,0:T(8,128)(2,1)} %k_ref.1, bf16[256,1024]{1,0:T(8,128)(2,1)} %v_ref.1, f32[8,256]{1,0:T(8,128)S(1)} %get-tuple-element.28.run_row_ref, ...), custom_call_target="tpu_custom_call" | custom-call | flops 268435456 | bytes 4210688 | tf_op jit(solution)/shard_map/pallas_call | solution.py:51
  18.0 14.7 %all-to-all-done = f32[32,1,4224]{2,1,0:T(1,128)S(1)} async-done(((f32[32,1,4224]{2,1,0:T(1,128)}), f32[32,1,4224]{2,1,0:T(1,128)S(1)}, u32[]{:S(2)}, u32[]{:S(2)}) %all-to-all-start) | async-done | bytes 540704 | tf_op jit(solution)/shard_map/all_to_all | solution.py:287
  32.8 1.2 collective-permute-done.refs_1_.refs_3_.refs_5_.refs_9_
  34.0 1.7 %collective-permute-start.3 = (f32[40,128]{1,0:T(8,128)S(1)}, f32[40,128]{1,0:T(8,128)S(1)}, u32[]{:S(2)}, u32[]{:S(2)}) collective-permute-start(f32[40,128]{1,0:T(8,128)S(1)} %shard_map.87), channel_id=1, source_target_pairs={{0,64},{64,128},{128,192},{192,0},{1,65},{65,129},{129,193},{193,1... | collective-permute-start | bytes 61448 | tf_op jit(solution)/shard_map/ppermute | solution.py:279
  35.7 2.9 %collective-permute-start.2 = (f32[40,128]{1,0:T(8,128)S(1)}, f32[40,128]{1,0:T(8,128)S(1)}, u32[]{:S(2)}, u32[]{:S(2)}) collective-permute-start(f32[40,128]{1,0:T(8,128)S(1)} %shard_map.87), channel_id=1, source_target_pairs={{0,128},{64,192},{128,0},{192,64},{1,129},{65,193},{129,1},{193,65... | collective-permute-start | bytes 61448 | tf_op jit(solution)/shard_map/ppermute | solution.py:279
  38.6 1.3 %collective-permute-start.1 = (f32[40,128]{1,0:T(8,128)S(1)}, f32[40,128]{1,0:T(8,128)S(1)}, u32[]{:S(2)}, u32[]{:S(2)}) collective-permute-start(f32[40,128]{1,0:T(8,128)S(1)} %shard_map.87), channel_id=1, source_target_pairs={{0,192},{64,0},{128,64},{192,128},{1,193},{65,1},{129,65},{193,129... | collective-permute-start | bytes 61448 | tf_op jit(solution)/shard_map/ppermute | solution.py:279
  39.9 1.0 collective-permute-done.2.refs_3_.refs_7_
  41.0 1.4 %collective-permute-done.1.refs_2_.refs_6_.refs_8_ = f32[40,128]{1,0:T(8,128)S(1)} collective-permute-done((f32[40,128]{1,0:T(8,128)S(1)}, f32[40,128]{1,0:T(8,128)S(1)}, u32[]{:S(2)}, u32[]{:S(2)}) %collective-permute-start.1) | collective-permute-done | bytes 20512 | tf_op jit(solution)/shard_map/ppermute | solution.py:279
  42.4 21.3 %all_to_all.20 = f32[32,32,128]{2,1,0:T(8,128)S(1)} all-to-all(f32[32,32,128]{2,1,0:T(8,128)S(1)} %shard_map.88), channel_id=1, replica_groups=mesh['y'=4,'core'=2,'x'=4,'z'=8] {'x','z'}, dimensions={0} | all-to-all | bytes 1048576 | tf_op jit(solution)/shard_map/all_to_all | solution.py:287
  63.8 2.1 %shard_map.89 = (bf16[256,1024]{1,0:T(8,128)(2,1)S(1)}, bf16[256,1024]{1,0:T(8,128)(2,1)S(1)}, f32[8,128,128]{2,1,0:T(8,128)}, bf16[8,128,128]{2,1,0:T(8,128)(2,1)}) custom-call(f32[256,1024]{1,0:T(8,128)S(1)} %get-tuple-element.34.mixed_ref, bf16[256,1024]{1,0:T(8,128)(2,1)S(1)} %get-tuple-element.35.query_dec_ref, bf16[256,1024]{1,0:T(8,128)(2,1)S(1)} %copy-done.3, ...), custom_call_target="tpu_custom_call" | custom-call | flops 134217728 | bytes 4456448 | tf_op jit(solution)/shard_map/pallas_call | solution.py:51
  65.9 5.0 %all-to-all-start.2 = ((f32[32,32,128]{2,1,0:T(8,128)}), f32[32,32,128]{2,1,0:T(8,128)S(1)}, u32[]{:S(2)}, u32[]{:S(2)}) async-start(f32[32,32,128]{2,1,0:T(8,128)} %bitcast.13), calls=%async_computation.2 | async-start | bytes 1048576 | tf_op jit(solution)/shard_map/all_to_all | solution.py:287
  70.9 5.4 %shard_map.90 = (bf16[256,1024]{1,0:T(8,128)(2,1)}, f32[256,1024]{1,0:T(8,128)S(1)}, f32[256,1024]{1,0:T(8,128)S(1)}, bf16[256,1024]{1,0:T(8,128)(2,1)}) custom-call(bf16[256,1024]{1,0:T(8,128)(2,1)} %q_hbm.3, bf16[256,1024]{1,0:T(8,128)(2,1)} %k_ref.1, bf16[256,1024]{1,0:T(8,128)(2,1)} %v_ref.1, bf16[8,256,256]{2,1,0:T(8,128)(2,1)} %get-tuple-element.30.weights_hbm, ...), custom_call_target="tpu_custom_call" | custom-call | flops 603979776 | bytes 7094272 | tf_op jit(solution)/shard_map/pallas_call | solution.py:51
  76.4 1.0 copy-done.2
  77.4 9.6 %all-to-all-done.2 = f32[32,32,128]{2,1,0:T(8,128)S(1)} async-done(((f32[32,32,128]{2,1,0:T(8,128)}), f32[32,32,128]{2,1,0:T(8,128)S(1)}, u32[]{:S(2)}, u32[]{:S(2)}) %all-to-all-start.2) | async-done | bytes 524320 | tf_op jit(solution)/shard_map/all_to_all | solution.py:287
  87.1 1.2 collective-permute-done.4.refs_1_.refs_5_
  88.3 1.6 %collective-permute-start.7 = (f32[32,128]{1,0:T(8,128)S(1)}, f32[32,128]{1,0:T(8,128)S(1)}, u32[]{:S(2)}, u32[]{:S(2)}) collective-permute-start(f32[32,128]{1,0:T(8,128)S(1)} %shard_map.92), channel_id=1, source_target_pairs={{0,192},{64,0},{128,64},{192,128},{1,193},{65,1},{129,65},{193,129... | collective-permute-start | bytes 49160 | tf_op jit(solution)/shard_map/ppermute | solution.py:279
  89.9 0.7 collective-permute-start.6
  90.7 0.7 collective-permute-start.5
  91.3 0.8 collective-permute-done.7.refs_4_
  92.1 3.1 %collective-permute-done.6.refs_3_ = f32[32,128]{1,0:T(8,128)S(1)} collective-permute-done((f32[32,128]{1,0:T(8,128)S(1)}, f32[32,128]{1,0:T(8,128)S(1)}, u32[]{:S(2)}, u32[]{:S(2)}) %collective-permute-start.6) | collective-permute-done | bytes 16416 | tf_op jit(solution)/shard_map/ppermute | solution.py:279
  95.7 21.0 %all_to_all.21 = f32[32,32,128]{2,1,0:T(8,128)S(1)} all-to-all(f32[32,32,128]{2,1,0:T(8,128)S(1)} %shard_map.93), channel_id=1, replica_groups=mesh['y'=4,'core'=2,'x'=4,'z'=8] {'x','z'}, dimensions={0} | all-to-all | bytes 1048576 | tf_op jit(solution)/shard_map/all_to_all | solution.py:287
  116.7 2.3 %shard_map.94 = (bf16[256,1024]{1,0:T(8,128)(2,1)}, bf16[256,1024]{1,0:T(8,128)(2,1)}) custom-call(bf16[256,1024]{1,0:T(8,128)(2,1)S(1)} %copy-done, bf16[256,1024]{1,0:T(8,128)(2,1)S(1)} %copy-done.1, f32[256,8]{1,0:T(8,128)S(1)} %get-tuple-element.29.run_col_ref, f32[256,1024]{1,0:T(8,128)S(1)} %get-tuple-element.47.part_k_ref, f32[256,1024]{1,0:T(8,128)} %copy-done.2, ...), custom_call_target="tpu_custom_call" | custom-call | flops 134217728 | bytes 4726784 | tf_op jit(solution)/shard_map/pallas_call | solution.py:51
  (19 shorter events, 1.0 us)
Async XLA Ops:
  3.5 29.1 %all-to-all-start = ((f32[32,1,4224]{2,1,0:T(1,128)}), f32[32,1,4224]{2,1,0:T(1,128)S(1)}, u32[]{:S(2)}, u32[]{:S(2)}) async-start(f32[32,1,4224]{2,1,0:T(1,128)} %bitcast.12), calls=%async_computation | async-start | bytes 1081344 | tf_op jit(solution)/shard_map/all_to_all | solution.py:287
  32.7 1.3 %collective-permute-start = (f32[40,128]{1,0:T(8,128)S(1)}, f32[40,128]{1,0:T(8,128)S(1)}, u32[]{:S(2)}, u32[]{:S(2)}) collective-permute-start(f32[40,128]{1,0:T(8,128)S(1)} %get-tuple-element.38.refs_0_.refs_2_), channel_id=1, source_target_pairs={{0,32},{32,0},{1,33},{33,1},{2,34},{34,2},{3,35},{35,3},{4,36},{36... | collective-permute-start | bytes 61448 | tf_op jit(solution)/shard_map/ppermute | solution.py:283
  34.0 5.9 %collective-permute-start.3 = (f32[40,128]{1,0:T(8,128)S(1)}, f32[40,128]{1,0:T(8,128)S(1)}, u32[]{:S(2)}, u32[]{:S(2)}) collective-permute-start(f32[40,128]{1,0:T(8,128)S(1)} %shard_map.87), channel_id=1, source_target_pairs={{0,64},{64,128},{128,192},{192,0},{1,65},{65,129},{129,193},{193,1... | collective-permute-start | bytes 61448 | tf_op jit(solution)/shard_map/ppermute | solution.py:279
  35.7 5.3 %collective-permute-start.2 = (f32[40,128]{1,0:T(8,128)S(1)}, f32[40,128]{1,0:T(8,128)S(1)}, u32[]{:S(2)}, u32[]{:S(2)}) collective-permute-start(f32[40,128]{1,0:T(8,128)S(1)} %shard_map.87), channel_id=1, source_target_pairs={{0,128},{64,192},{128,0},{192,64},{1,129},{65,193},{129,1},{193,65... | collective-permute-start | bytes 61448 | tf_op jit(solution)/shard_map/ppermute | solution.py:279
  38.6 3.8 %collective-permute-start.1 = (f32[40,128]{1,0:T(8,128)S(1)}, f32[40,128]{1,0:T(8,128)S(1)}, u32[]{:S(2)}, u32[]{:S(2)}) collective-permute-start(f32[40,128]{1,0:T(8,128)S(1)} %shard_map.87), channel_id=1, source_target_pairs={{0,192},{64,0},{128,64},{192,128},{1,193},{65,1},{129,65},{193,129... | collective-permute-start | bytes 61448 | tf_op jit(solution)/shard_map/ppermute | solution.py:279
  42.4 21.4 %copy-start.3 = (bf16[256,1024]{1,0:T(8,128)(2,1)S(1)}, bf16[256,1024]{1,0:T(8,128)(2,1)}, u32[]{:S(2)}) copy-start(bf16[256,1024]{1,0:T(8,128)(2,1)} %g_ref.1) | copy-start | bytes 1572868
  65.9 5.0 %copy-start.4 = (bf16[8,128,128]{2,1,0:T(8,128)(2,1)S(1)}, bf16[8,128,128]{2,1,0:T(8,128)(2,1)}, u32[]{:S(2)}) copy-start(bf16[8,128,128]{2,1,0:T(8,128)(2,1)} %get-tuple-element.40.half_ref) | copy-start | bytes 786436
  65.9 21.0 %all-to-all-start.2 = ((f32[32,32,128]{2,1,0:T(8,128)}), f32[32,32,128]{2,1,0:T(8,128)S(1)}, u32[]{:S(2)}, u32[]{:S(2)}) async-start(f32[32,32,128]{2,1,0:T(8,128)} %bitcast.13), calls=%async_computation.2 | async-start | bytes 1048576 | tf_op jit(solution)/shard_map/all_to_all | solution.py:287
  76.4 1.0 copy-start.2
  87.0 1.3 %collective-permute-start.4 = (f32[32,128]{1,0:T(8,128)S(1)}, f32[32,128]{1,0:T(8,128)S(1)}, u32[]{:S(2)}, u32[]{:S(2)}) collective-permute-start(f32[32,128]{1,0:T(8,128)S(1)} %shard_map.91.refs_0_), channel_id=1, source_target_pairs={{0,32},{32,0},{1,33},{33,1},{2,34},{34,2},{3,35},{35,3},{4,36},{36... | collective-permute-start | bytes 49160 | tf_op jit(solution)/shard_map/ppermute | solution.py:283
  88.3 3.8 %collective-permute-start.7 = (f32[32,128]{1,0:T(8,128)S(1)}, f32[32,128]{1,0:T(8,128)S(1)}, u32[]{:S(2)}, u32[]{:S(2)}) collective-permute-start(f32[32,128]{1,0:T(8,128)S(1)} %shard_map.92), channel_id=1, source_target_pairs={{0,192},{64,0},{128,64},{192,128},{1,193},{65,1},{129,65},{193,129... | collective-permute-start | bytes 49160 | tf_op jit(solution)/shard_map/ppermute | solution.py:279
  89.9 5.2 %collective-permute-start.6 = (f32[32,128]{1,0:T(8,128)S(1)}, f32[32,128]{1,0:T(8,128)S(1)}, u32[]{:S(2)}, u32[]{:S(2)}) collective-permute-start(f32[32,128]{1,0:T(8,128)S(1)} %shard_map.92), channel_id=1, source_target_pairs={{0,128},{64,192},{128,0},{192,64},{1,129},{65,193},{129,1},{193,65... | collective-permute-start | bytes 49160 | tf_op jit(solution)/shard_map/ppermute | solution.py:279
  90.7 4.9 %collective-permute-start.5 = (f32[32,128]{1,0:T(8,128)S(1)}, f32[32,128]{1,0:T(8,128)S(1)}, u32[]{:S(2)}, u32[]{:S(2)}) collective-permute-start(f32[32,128]{1,0:T(8,128)S(1)} %shard_map.92), channel_id=1, source_target_pairs={{0,64},{64,128},{128,192},{192,0},{1,65},{65,129},{129,193},{193,1... | collective-permute-start | bytes 49160 | tf_op jit(solution)/shard_map/ppermute | solution.py:279
  95.7 21.0 %copy-start = (bf16[256,1024]{1,0:T(8,128)(2,1)S(1)}, bf16[256,1024]{1,0:T(8,128)(2,1)}, u32[]{:S(2)}) copy-start(bf16[256,1024]{1,0:T(8,128)(2,1)} %k_ref.1) | copy-start | bytes 1572868
  95.7 21.0 %copy-start.1 = (bf16[256,1024]{1,0:T(8,128)(2,1)S(1)}, bf16[256,1024]{1,0:T(8,128)(2,1)}, u32[]{:S(2)}) copy-start(bf16[256,1024]{1,0:T(8,128)(2,1)} %v_ref.1) | copy-start | bytes 1572868
